TPU v7x, 256 devices: a whole 4x4x8 slice. The times are simulated.
256 devices in a mesh: gx: 16 (over x, z_hi), gy: 16 (over z_lo, y, core).
Axes of the slice: x: 4, y: 4, z: 8 (z_hi: 4, z_lo: 2; z = z_hi * 2 + z_lo), core: 2. Of those that a mesh axis runs over, the one named last changes fastest.
Arguments:
- field: bfloat16 [20, 32, 64, 512], P(None, 'gx', 'gy'), may hold values from -6 to 6
- cotangent: bfloat16 [20, 32, 64, 512], P(None, 'gx', 'gy'), may hold values from -6 to 6
- spectral_weight: float32 [64, 2, 20, 20, 16, 16], P('gx', None, None, None, 'gy'), may hold values from -3 to 3
- pointwise_weight: bfloat16 [20, 20], replicated, may hold values from -1.25 to 1.25
- channel_bias: float32 [20], replicated, may hold values from -3 to 3
Outputs:
- layer_out: bfloat16 [20, 32, 64, 512], P(None, 'gx', 'gy')
- grad_field: bfloat16 [20, 32, 64, 512], P(None, 'gx', 'gy')
- grad_spectral: float32 [64, 2, 20, 20, 16, 16], P('gx', None, None, None, 'gy')
All inputs are finite; a program needn't handle non-finite values.
Results may differ from a plain program's by a relative error of at most 0.0061.
Values sent between devices are 32-bit elements; how exact they have to be, the bound alone decides.
A program may use at most 64 MiB of HBM per device.

v0:
```python
import math

import jax
import jax.numpy as jnp
from jax import lax
from jax.sharding import PartitionSpec as P

KX = 16
KY = 16
KZ = 16
KT = 4
NZ = 32
NT = 16


HIGHEST_PRECISION = lax.Precision.HIGHEST


def rotation(length, kept_modes, phase_sign, cell_count, offset):
    position = offset + jnp.arange(cell_count, dtype=jnp.int32)
    mode_index = jnp.arange(kept_modes, dtype=jnp.int32)
    frequency = jnp.where(mode_index < kept_modes // 2, mode_index, mode_index - kept_modes)
    phase_int = jnp.mod(position[:, None] * frequency[None, :], length)
    angles = phase_int.astype(jnp.float32) * (phase_sign * 2.0 * math.pi / length)
    factor = 1.0 / math.sqrt(length)
    cosine = jnp.cos(angles) * factor
    sine_part = jnp.sin(angles) * factor
    return jnp.stack([jnp.stack([cosine, sine_part]), jnp.stack([-sine_part, cosine])])


def depth_time_table(depth_cells, time_cells, modes_depth, modes_time):
    depth_pos = jnp.arange(depth_cells, dtype=jnp.int32)
    time_pos = jnp.arange(time_cells, dtype=jnp.int32)
    depth_index = jnp.arange(modes_depth, dtype=jnp.int32)
    depth_freq = jnp.where(depth_index < modes_depth // 2, depth_index, depth_index - modes_depth)
    time_freq = jnp.arange(modes_time, dtype=jnp.int32)
    total_cells = depth_cells * time_cells
    phase_int = (
        depth_pos[:, None, None, None] * depth_freq[None, None, :, None] * time_cells
        + time_pos[None, :, None, None] * time_freq[None, None, None, :] * depth_cells
    )
    phase_int = jnp.mod(phase_int, total_cells).reshape(total_cells, modes_depth * modes_time)
    angles = phase_int.astype(jnp.float32) * (2.0 * math.pi / total_cells)
    factor = 1.0 / math.sqrt(total_cells)
    return jnp.stack([jnp.cos(angles) * factor, -jnp.sin(angles) * factor], axis=1)


def mode_weight(first_mode, mode_count, modes_time):
    mode_ids = first_mode + jnp.arange(mode_count, dtype=jnp.int32)
    weights = jnp.where(jnp.mod(mode_ids, modes_time) == 0, 1.0, 2.0).astype(jnp.float32)
    return weights.reshape(mode_count, 1, 1, 1, 1)


def mix_pair(left_part, right_part):
    return jnp.einsum("mwkj,mwokj->mokj", left_part, right_part, precision=HIGHEST_PRECISION)


def adjoint_pair(left_part, right_part):
    return jnp.einsum("mwokj,mokj->mwkj", left_part, right_part, precision=HIGHEST_PRECISION)


def complex_mix(spectra, weights):
    real_in, imag_in = (spectra[:, 0], spectra[:, 1])
    real_w, imag_w = (weights[:, 0], weights[:, 1])
    real_out = mix_pair(real_in, real_w) - mix_pair(imag_in, imag_w)
    imag_out = mix_pair(real_in, imag_w) + mix_pair(imag_in, real_w)
    return jnp.stack([real_out, imag_out], axis=1)


def adjoint_mix(weights, spectra):
    real_w, imag_w = (weights[:, 0], weights[:, 1])
    real_in, imag_in = (spectra[:, 0], spectra[:, 1])
    real_out = adjoint_pair(real_w, real_in) + adjoint_pair(imag_w, imag_in)
    imag_out = adjoint_pair(real_w, imag_in) - adjoint_pair(imag_w, real_in)
    return jnp.stack([real_out, imag_out], axis=1)


def weight_grad(inputs, outputs):
    real_in = inputs[:, 0][:, :, None]
    imag_in = inputs[:, 1][:, :, None]
    real_out = outputs[:, 0][:, None]
    imag_out = outputs[:, 1][:, None]
    real_part = real_in * real_out + imag_in * imag_out
    imag_part = real_in * imag_out - imag_in * real_out
    return jnp.stack([real_part, imag_part], axis=1)


def on_device(field, cotangent, spectral_weight, pointwise_weight, channel_bias):
    cells_first = field.shape[1]
    cells_second = field.shape[2]
    length_first = cells_first * lax.axis_size("gx")
    length_second = cells_second * lax.axis_size("gy")
    local_modes = spectral_weight.shape[0]
    block_start = lax.axis_index("gx") * cells_first
    weights_modes = mode_weight(lax.axis_index("gx") * local_modes, local_modes, KT)
    table_float = depth_time_table(NZ, NT, KZ, KT)
    table_half = table_float.astype(jnp.bfloat16)
    forward_block = rotation(length_first, KX, -1.0, cells_first, block_start)
    forward_second = rotation(length_second, KY, -1.0, length_second, 0)
    inverse_block = rotation(length_first, KX, 1.0, cells_first, block_start)
    inverse_second = rotation(length_second, KY, 1.0, length_second, 0)

    def transform_second(pencil):
        return jnp.einsum("mswky,sryj->mrwkj", pencil, forward_second, precision=HIGHEST_PRECISION)

    def finish_cells(pencil):
        return jnp.einsum("msoyx,qsm->oxyq", pencil, table_float, precision=HIGHEST_PRECISION)

    def partial_inverse(pencil):
        return jnp.einsum("msoky,srxk->mroyx", pencil, inverse_block, precision=HIGHEST_PRECISION)

    def forward_spectrum(values):
        first_section = jnp.einsum(
            "wxyq,qsm->mswyx", values, table_half, preferred_element_type=jnp.float32
        )
        second_section = lax.psum_scatter(
            jnp.einsum(
                "mswyx,srxk->mrwky", first_section, forward_block, precision=HIGHEST_PRECISION
            ),
            "gx",
            scatter_dimension=0,
            tiled=True,
        )
        return transform_second(
            lax.all_to_all(second_section, "gy", split_axis=3, concat_axis=4, tiled=True)
        )

    def inverse_cells(spectra):
        first_section = jnp.einsum(
            "msokj,sryj->mroky", spectra, inverse_second, precision=HIGHEST_PRECISION
        )
        returned = lax.all_to_all(first_section, "gy", split_axis=4, concat_axis=3, tiled=True)
        gathered = partial_inverse(lax.all_gather(returned, "gx", axis=0, tiled=True))
        spatial = finish_cells(gathered)
        return spatial

    spectra = forward_spectrum(field)
    mixed_modes = complex_mix(spectra, spectral_weight) * weights_modes
    spatial = inverse_cells(mixed_modes)
    local_term = jnp.einsum(
        "wo,wxyq->oxyq", pointwise_weight, field, preferred_element_type=jnp.float32
    )
    pre_act = spatial + local_term + channel_bias[:, None, None, None]
    activated, pullback = jax.vjp(jax.nn.gelu, pre_act)
    signal = pullback(cotangent.astype(jnp.float32))[0].astype(jnp.bfloat16)
    layer_out = activated.astype(jnp.bfloat16)
    back_spectra = forward_spectrum(signal) * weights_modes
    grad_spectral = weight_grad(spectra, back_spectra)
    back_cells = inverse_cells(adjoint_mix(spectral_weight, back_spectra))
    back_local = jnp.einsum(
        "wo,oxyq->wxyq", pointwise_weight, signal, preferred_element_type=jnp.float32
    )
    grad_field = (back_cells + back_local).astype(jnp.bfloat16)
    return (layer_out, grad_field, grad_spectral)


def solution(mesh):
    return jax.shard_map(
        on_device,
        mesh=mesh,
        in_specs=(
            P(None, "gx", "gy", None),
            P(None, "gx", "gy", None),
            P("gx", None, None, None, "gy", None),
            P(),
            P(),
        ),
        out_specs=(
            P(None, "gx", "gy", None),
            P(None, "gx", "gy", None),
            P("gx", None, None, None, "gy", None),
        ),
        check_vma=False,
    )
```

profile of v0, /device:TPU:1, one launch (start us, length us, event | category | flops | bytes accessed | tf_op | source)
XLA Modules:
  0.0 553.3 jit_solution(6807744942063237344)
XLA Ops:
  10.0 1.3 convolution_bitcast_fusion.1
  11.3 4.6 copy.51
  18.7 96.5 %reduce-scatter.3.cloned.1.call-done = f32[4,2,20,16,4]{2,3,4,1,0:T(8,128)} async-done(((f32[64,2,20,16,4]{2,3,4,1,0:T(8,128)}), f32[4,2,20,16,4]{2,3,4,1,0:T(8,128)}) %reduce-scatter.3.cloned.1.call-update) | async-done | bytes 40976 | tf_op jit(solution)/shard_map/reduce_scatter | solution.py:116
  117.1 6.3 %all-to-all-start = ((f32[16,1,640]{2,1,0:T(1,128)}), f32[16,1,640]{2,1,0:T(1,128)S(1)}, u32[]{:S(2)}, u32[]{:S(2)}) async-start(f32[16,1,640]{2,1,0:T(1,128)} %reshape.890), calls=%async_computation.1 | async-start | bytes 81920 | tf_op jit(solution)/shard_map/all_to_all | solution.py:125
  123.5 5.8 %all-to-all-done = f32[16,1,640]{2,1,0:T(1,128)S(1)} async-done(((f32[16,1,640]{2,1,0:T(1,128)}), f32[16,1,640]{2,1,0:T(1,128)S(1)}, u32[]{:S(2)}, u32[]{:S(2)}) %all-to-all-start) | async-done | bytes 40992 | tf_op jit(solution)/shard_map/all_to_all | solution.py:125
  131.9 1.3 fusion.80
  133.2 1.3 fusion.82
  134.6 1.3 fusion.81
  135.9 1.3 fusion.83
  138.8 3.7 all-to-all-start.1
  142.5 5.8 %all-to-all-done.1 = f32[16,1,640]{2,1,0:T(1,128)S(1)} async-done(((f32[16,1,640]{2,1,0:T(1,128)}), f32[16,1,640]{2,1,0:T(1,128)S(1)}, u32[]{:S(2)}, u32[]{:S(2)}) %all-to-all-start.1) | async-done | bytes 40992 | tf_op jit(solution)/shard_map/all_to_all | solution.py:132
  149.6 104.3 %all_gather.6 = f32[64,2,20,16,4]{2,3,4,1,0:T(8,128)} all-gather(f32[4,2,20,16,4]{2,3,4,1,0:T(8,128)S(1)} %copy.58), channel_id=1, replica_groups=mesh['gx'=16,'gy'=16] {'gx'}, dimensions={0}, use_global_device_ids=true | all-gather | bytes 696320 | tf_op jit(solution)/shard_map/all_gather | solution.py:133
  253.9 7.6 %copy.59 = f32[64,2,20,16,4]{3,0,1,4,2:T(8,128)} copy(f32[64,2,20,16,4]{2,3,4,1,0:T(8,128)} %all_gather.6) | data formatting | bytes 1310720 | tf_op jit(solution)/shard_map/all_gather | solution.py:133
  261.5 14.5 %fusion.7 = f32[64,2,20,4,2]{0,4,3,2,1:T(2,128)S(1)} fusion(f32[64,2,20,16,4]{3,0,1,4,2:T(8,128)} %copy.59, f32[1,2,2,16]{3,2,0,1:T(2,128)S(1)} %get-tuple-element.33, f32[1,2,2,16]{3,2,0,1:T(2,128)S(1)} %get-tuple-element.32), kind=kOutput, calls=%fused_computation.16 | convolution fusion | flops 7864448 | bytes 737792 | tf_op jit(solution)/shard_map/msoky,srxk->mroyx/dot_general | solution.py:110
  277.4 1.3 convolution_bitcast_fusion
  278.7 4.6 copy.67
  283.4 102.5 %reduce-scatter.5.cloned.1.call-done = f32[4,2,20,16,4]{2,3,4,1,0:T(8,128)} async-done(((f32[64,2,20,16,4]{2,3,4,1,0:T(8,128)}), f32[4,2,20,16,4]{2,3,4,1,0:T(8,128)}) %reduce-scatter.5.cloned.1.call-update) | async-done | bytes 40976 | tf_op jit(solution)/shard_map/reduce_scatter | solution.py:116
  387.9 6.3 %all-to-all-start.2 = ((f32[16,1,640]{2,1,0:T(1,128)}), f32[16,1,640]{2,1,0:T(1,128)S(1)}, u32[]{:S(2)}, u32[]{:S(2)}) async-start(f32[16,1,640]{2,1,0:T(1,128)} %reshape.894), calls=%async_computation.4 | async-start | bytes 81920 | tf_op jit(solution)/shard_map/all_to_all | solution.py:125
  395.2 4.8 all-to-all-done.2
  406.4 3.7 all-to-all-start.3
  411.7 4.3 all-to-all-done.3
  417.2 105.6 %all_gather.7 = f32[64,2,20,16,4]{2,3,4,1,0:T(8,128)} all-gather(f32[4,2,20,16,4]{2,3,4,1,0:T(8,128)S(1)} %copy.74), channel_id=1, replica_groups=mesh['gx'=16,'gy'=16] {'gx'}, dimensions={0}, use_global_device_ids=true | all-gather | bytes 696320 | tf_op jit(solution)/shard_map/all_gather | solution.py:133
  522.9 7.6 %copy.75 = f32[64,2,20,16,4]{3,0,1,4,2:T(8,128)} copy(f32[64,2,20,16,4]{2,3,4,1,0:T(8,128)} %all_gather.7) | data formatting | bytes 1310720 | tf_op jit(solution)/shard_map/all_gather | solution.py:133
  530.5 14.5 %fusion.10 = f32[64,2,20,4,2]{0,4,3,2,1:T(2,128)S(1)} fusion(f32[64,2,20,16,4]{3,0,1,4,2:T(8,128)} %copy.75, f32[1,2,2,16]{3,2,0,1:T(2,128)S(1)} %copy-done.16, f32[1,2,2,16]{3,2,0,1:T(2,128)S(1)} %copy-done.14), kind=kOutput, calls=%fused_computation.17 | convolution fusion | flops 7864448 | bytes 737792 | tf_op jit(solution)/shard_map/msoky,srxk->mroyx/dot_general | solution.py:110
  (109 shorter events, 27.7 us)
Async XLA Ops:
  7.2 269.4 %copy-start = (bf16[20,20]{1,0:T(8,128)(2,1)S(1)}, bf16[20,20]{1,0:T(8,128)(2,1)}, u32[]{:S(2)}) copy-start(bf16[20,20]{1,0:T(8,128)(2,1)} %param.8) | copy-start | bytes 2404
  7.2 108.0 %reduce-scatter.3.cloned.1.call-start = ((), (), s32[]{:S(2)}) async-start(), calls=%async_computation.6 | async-start | bytes 4456448 | tf_op jit(solution)/shard_map/reduce_scatter | solution.py:116
  18.6 235.3 %copy-start.7 = (f32[1,2,64,16]{2,3,0,1:T(8,128)}, f32[1,2,64,16]{2,3,0,1:T(8,128)S(1)}, u32[]{:S(2)}) copy-start(f32[1,2,64,16]{2,3,0,1:T(8,128)S(1)} %get-tuple-element.30) | copy-start | bytes 24580
  18.6 235.2 %copy-start.9 = (f32[1,2,64,16]{2,3,0,1:T(8,128)}, f32[1,2,64,16]{2,3,0,1:T(8,128)S(1)}, u32[]{:S(2)}) copy-start(f32[1,2,64,16]{2,3,0,1:T(8,128)S(1)} %get-tuple-element.31) | copy-start | bytes 24580
  18.7 235.2 %copy-start.3 = (f32[1,2,64,16]{2,3,1,0:T(8,128)}, f32[1,2,64,16]{2,3,1,0:T(8,128)S(1)}, u32[]{:S(2)}) copy-start(f32[1,2,64,16]{2,3,1,0:T(8,128)S(1)} %get-tuple-element.28) | copy-start | bytes 24580
  18.7 235.2 %copy-start.5 = (f32[1,2,64,16]{2,3,1,0:T(8,128)}, f32[1,2,64,16]{2,3,1,0:T(8,128)S(1)}, u32[]{:S(2)}) copy-start(f32[1,2,64,16]{2,3,1,0:T(8,128)S(1)} %get-tuple-element.29) | copy-start | bytes 24580
  117.1 12.1 %all-to-all-start = ((f32[16,1,640]{2,1,0:T(1,128)}), f32[16,1,640]{2,1,0:T(1,128)S(1)}, u32[]{:S(2)}, u32[]{:S(2)}) async-start(f32[16,1,640]{2,1,0:T(1,128)} %reshape.890), calls=%async_computation.1 | async-start | bytes 81920 | tf_op jit(solution)/shard_map/all_to_all | solution.py:125
  123.5 19.0 %copy-start.17 = (f32[4]{0:T(128)}, f32[4]{0:T(128)S(1)}, u32[]{:S(2)}) copy-start(f32[4]{0:T(128)S(1)} %compare_select_fusion.5) | copy-start | bytes 52
  138.8 9.6 %all-to-all-start.1 = ((f32[16,1,640]{2,1,0:T(1,128)}), f32[16,1,640]{2,1,0:T(1,128)S(1)}, u32[]{:S(2)}, u32[]{:S(2)}) async-start(f32[16,1,640]{2,1,0:T(1,128)} %reshape.892), calls=%async_computation.2 | async-start | bytes 81920 | tf_op jit(solution)/shard_map/all_to_all | solution.py:132
  142.4 243.5 %reduce-scatter.5.cloned.1.call-start = ((), (), s32[]{:S(2)}) async-start(), calls=%async_computation.7 | async-start | bytes 4456448 | tf_op jit(solution)/shard_map/reduce_scatter | solution.py:116
  142.5 119.0 %copy-start.13 = (f32[1,2,2,16]{3,2,0,1:T(2,128)}, f32[1,2,2,16]{3,2,0,1:T(2,128)S(1)}, u32[]{:S(2)}) copy-start(f32[1,2,2,16]{3,2,0,1:T(2,128)S(1)} %get-tuple-element.32) | copy-start | bytes 772
  142.5 119.0 %copy-start.15 = (f32[1,2,2,16]{3,2,0,1:T(2,128)}, f32[1,2,2,16]{3,2,0,1:T(2,128)S(1)}, u32[]{:S(2)}) copy-start(f32[1,2,2,16]{3,2,0,1:T(2,128)S(1)} %get-tuple-element.33) | copy-start | bytes 772
  261.5 15.1 %copy-start.2 = (bf16[20,2,4,512]{3,2,1,0:T(4,128)(2,1)S(1)}, bf16[20,2,4,512]{3,2,1,0:T(4,128)(2,1)}, u32[]{:S(2)}) copy-start(bf16[20,2,4,512]{3,2,1,0:T(4,128)(2,1)} %param.5) | copy-start | bytes 491524
  261.5 15.1 %copy-start.19 = (bf16[20,2,4,512]{3,2,1,0:T(4,128)(2,1)S(1)}, bf16[20,2,4,512]{3,2,1,0:T(4,128)(2,1)}, u32[]{:S(2)}) copy-start(bf16[20,2,4,512]{3,2,1,0:T(4,128)(2,1)} %param.6) | copy-start | bytes 491524
  261.5 15.1 %copy-start.20 = (f32[20]{0:T(128)S(1)}, f32[20]{0:T(128)}, u32[]{:S(2)}) copy-start(f32[20]{0:T(128)} %param.9) | copy-start | bytes 244
  283.4 110.8 %copy-start.12 = (f32[4,20,16]{1,2,0:T(8,128)S(1)}, f32[4,20,16]{1,2,0:T(8,128)}, u32[]{:S(2)}) copy-start(f32[4,20,16]{1,2,0:T(8,128)} %get-tuple-element.20) | copy-start | bytes 15364
  283.4 110.9 %copy-start.11 = (f32[4,20,16]{1,2,0:T(8,128)S(1)}, f32[4,20,16]{1,2,0:T(8,128)}, u32[]{:S(2)}) copy-start(f32[4,20,16]{1,2,0:T(8,128)} %get-tuple-element.21) | copy-start | bytes 15364
  283.4 117.8 %copy-start.8 = (f32[1,2,64,16]{2,3,0,1:T(8,128)S(1)}, f32[1,2,64,16]{2,3,0,1:T(8,128)}, u32[]{:S(2)}) copy-start(f32[1,2,64,16]{2,3,0,1:T(8,128)} %copy-done.7) | copy-start | bytes 24580
  283.4 117.8 %copy-start.10 = (f32[1,2,64,16]{2,3,0,1:T(8,128)S(1)}, f32[1,2,64,16]{2,3,0,1:T(8,128)}, u32[]{:S(2)}) copy-start(f32[1,2,64,16]{2,3,0,1:T(8,128)} %copy-done.9) | copy-start | bytes 24580
  283.4 117.8 %copy-start.18 = (f32[4]{0:T(128)S(1)}, f32[4]{0:T(128)}, u32[]{:S(2)}) copy-start(f32[4]{0:T(128)} %copy-done.17) | copy-start | bytes 52
  283.4 121.5 %copy-start.4 = (f32[1,2,64,16]{2,3,1,0:T(8,128)S(1)}, f32[1,2,64,16]{2,3,1,0:T(8,128)}, u32[]{:S(2)}) copy-start(f32[1,2,64,16]{2,3,1,0:T(8,128)} %copy-done.3) | copy-start | bytes 24580
  283.4 121.5 %copy-start.6 = (f32[1,2,64,16]{2,3,1,0:T(8,128)S(1)}, f32[1,2,64,16]{2,3,1,0:T(8,128)}, u32[]{:S(2)}) copy-start(f32[1,2,64,16]{2,3,1,0:T(8,128)} %copy-done.5) | copy-start | bytes 24580
  387.9 12.1 %all-to-all-start.2 = ((f32[16,1,640]{2,1,0:T(1,128)}), f32[16,1,640]{2,1,0:T(1,128)S(1)}, u32[]{:S(2)}, u32[]{:S(2)}) async-start(f32[16,1,640]{2,1,0:T(1,128)} %reshape.894), calls=%async_computation.4 | async-start | bytes 81920 | tf_op jit(solution)/shard_map/all_to_all | solution.py:125
  406.4 9.6 %all-to-all-start.3 = ((f32[16,1,640]{2,1,0:T(1,128)}), f32[16,1,640]{2,1,0:T(1,128)S(1)}, u32[]{:S(2)}, u32[]{:S(2)}) async-start(f32[16,1,640]{2,1,0:T(1,128)} %reshape.896), calls=%async_computation.5 | async-start | bytes 81920 | tf_op jit(solution)/shard_map/all_to_all | solution.py:132
  (3 other events, 16.6 us)
Sparse Core Ops, SparseCore 0:
  16.1 98.9 reduce-scatter.2
  283.5 102.3 reduce-scatter.4
where the time goes:
time: 560 us; the launch traced here: 553 us
  waiting for transfers between devices  220 us (39%)
  blocking collectives  210 us (38%)
  matrix products  44.7 us (8%)
  local copies, waits for them, and re-layouts  38.7 us (7%)
  starting transfers between devices  20.1 us (4%)
  between operations  14.6 us (3%)
  other arithmetic  5.68 us (1%)
    all_gather x2, blocking collectives, inverse_cells(): lax.all_gather(returned, 'gx', axis=0, tiled=True)  210 us
    reduce_scatter x2, waiting for transfers between devices, forward_spectrum(): lax.psum_scatter(jnp.einsum('mswyx,srxk->mrwky', first_section, forward_b...  199 us
    dot_general x2, matrix products, partial_inverse(): jnp.einsum('msoky,srxk->mroyx', pencil, inverse_block, precision=HIGHEST_...  29 us
    all_gather x2, local copies, waits for them, and re-layouts, inverse_cells(): lax.all_gather(returned, 'gx', axis=0, tiled=True)  15.2 us
    all_to_all x2, starting transfers between devices, forward_spectrum(): lax.all_to_all(second_section, 'gy', split_axis=3, concat_axis=4, tiled=T...  12.6 us
  transfers between devices with their start and end apart: 6, of which 6 were waited for; matrix products, arithmetic and copies ran while one was open for 1% of the time, Pallas kernels for 0%

commit v1 on v0

--- a/solution.py
+++ b/solution.py
@@ -91,13 +91,12 @@
     length_first = cells_first * lax.axis_size("gx")
     length_second = cells_second * lax.axis_size("gy")
     local_modes = spectral_weight.shape[0]
-    block_start = lax.axis_index("gx") * cells_first
     weights_modes = mode_weight(lax.axis_index("gx") * local_modes, local_modes, KT)
     table_float = depth_time_table(NZ, NT, KZ, KT)
     table_half = table_float.astype(jnp.bfloat16)
-    forward_block = rotation(length_first, KX, -1.0, cells_first, block_start)
+    forward_block = rotation(length_first, KX, -1.0, length_first, 0)
     forward_second = rotation(length_second, KY, -1.0, length_second, 0)
-    inverse_block = rotation(length_first, KX, 1.0, cells_first, block_start)
+    inverse_block = rotation(length_first, KX, 1.0, length_first, 0)
     inverse_second = rotation(length_second, KY, 1.0, length_second, 0)
 
     def transform_second(pencil):
@@ -113,13 +112,9 @@
         first_section = jnp.einsum(
             "wxyq,qsm->mswyx", values, table_half, preferred_element_type=jnp.float32
         )
-        second_section = lax.psum_scatter(
-            jnp.einsum(
-                "mswyx,srxk->mrwky", first_section, forward_block, precision=HIGHEST_PRECISION
-            ),
-            "gx",
-            scatter_dimension=0,
-            tiled=True,
+        gathered_x = lax.all_to_all(first_section, "gx", split_axis=0, concat_axis=4, tiled=True)
+        second_section = jnp.einsum(
+            "mswyx,srxk->mrwky", gathered_x, forward_block, precision=HIGHEST_PRECISION
         )
         return transform_second(
             lax.all_to_all(second_section, "gy", split_axis=3, concat_axis=4, tiled=True)
@@ -130,7 +125,9 @@
             "msokj,sryj->mroky", spectra, inverse_second, precision=HIGHEST_PRECISION
         )
         returned = lax.all_to_all(first_section, "gy", split_axis=4, concat_axis=3, tiled=True)
-        gathered = partial_inverse(lax.all_gather(returned, "gx", axis=0, tiled=True))
+        gathered = lax.all_to_all(
+            partial_inverse(returned), "gx", split_axis=4, concat_axis=0, tiled=True
+        )
         spatial = finish_cells(gathered)
         return spatial
 

time: 560 us -> 147 us (0.26); the launches traced: 553 us -> 146 us
  blocking collectives: 210 us -> 11.8 us
  waiting for transfers between devices: 220 us -> 45.9 us
  matrix products: 44.7 us -> 15.5 us
  starting transfers between devices: 20.1 us -> 38.6 us
  local copies, waits for them, and re-layouts: 38.7 us -> 23.7 us
  between operations: 14.6 us -> 1.4 us
    all_gather x2 -> x0, blocking collectives: 210 us -> none  [inverse_cells(): lax.all_gather(returned, 'gx', axis=0, tiled=True)]
    reduce_scatter x2 -> x0, waiting for transfers between devices: 199 us -> none  [forward_spectrum(): lax.psum_scatter(jnp.einsum('mswyx,srxk->mrwky', first_section, forward_b...]
    dot_general x2, matrix products: 29 us -> 1.3 us  [partial_inverse(): jnp.einsum('msoky,srxk->mroyx', pencil, inverse_block, precision=HIGHEST_...]
    all_to_all x0 -> x3, waiting for transfers between devices: none -> 23.7 us  [the longest x2 17.4 us: inverse_cells(): lax.all_to_all(partial_inverse(returned), 'gx', split_axis=4, concat_axis...]
    all_to_all x0 -> x3, starting transfers between devices: none -> 18.6 us  [the longest x1 11.6 us: forward_spectrum(): lax.all_to_all(first_section, 'gx', split_axis=0, concat_axis=4, tiled=True)]
    all_gather x2 -> x0, local copies, waits for them, and re-layouts: 15.2 us -> none  [inverse_cells(): lax.all_gather(returned, 'gx', axis=0, tiled=True)]
    all_to_all x0 -> x1, blocking collectives: none -> 11.8 us  [forward_spectrum(): lax.all_to_all(first_section, 'gx', split_axis=0, concat_axis=4, tiled=True)]
    transpose x2 -> x6, local copies, waits for them, and re-layouts: 9.3 us -> 2.1 us  [the longest x2 1.17 us: partial_inverse(): jnp.einsum('msoky,srxk->mroyx', pencil, inverse_block, precision=HIGHEST_...]
  transfers between devices with their start and end apart: 6 -> 7, of which waited for: 6 -> 7; matrix products, arithmetic and copies ran while one was open for 1% -> 4% of each run, Pallas kernels for 0% -> 0%
where the time goes in v1:
time: 147 us; the launch traced here: 146 us
  waiting for transfers between devices  45.9 us (31%)
  starting transfers between devices  38.6 us (26%)
  local copies, waits for them, and re-layouts  23.7 us (16%)
  matrix products  15.5 us (11%)
  blocking collectives  11.8 us (8%)
  other arithmetic  9.31 us (6%)
    all_to_all x2, waiting for transfers between devices, inverse_cells(): lax.all_to_all(partial_inverse(returned), 'gx', split_axis=4, concat_axis...  17.4 us
    unnamed x54, local copies, waits for them, and re-layouts  14.2 us
    all_to_all x2, starting transfers between devices, forward_spectrum(): lax.all_to_all(second_section, 'gy', split_axis=3, concat_axis=4, tiled=T...  12.6 us
    all_to_all x1, blocking collectives, forward_spectrum(): lax.all_to_all(first_section, 'gx', split_axis=0, concat_axis=4, tiled=True)  11.8 us
    all_to_all x1, starting transfers between devices, forward_spectrum(): lax.all_to_all(first_section, 'gx', split_axis=0, concat_axis=4, tiled=True)  11.6 us
    all_to_all x2, waiting for transfers between devices, forward_spectrum(): lax.all_to_all(second_section, 'gy', split_axis=3, concat_axis=4, tiled=T...  11.5 us
    all_to_all x2, waiting for transfers between devices, inverse_cells(): lax.all_to_all(first_section, 'gy', split_axis=4, concat_axis=3, tiled=True)  10.7 us
    all_to_all x2, starting transfers between devices, inverse_cells(): lax.all_to_all(first_section, 'gy', split_axis=4, concat_axis=3, tiled=True)  7.36 us
  transfers between devices with their start and end apart: 7, of which 7 were waited for; matrix products, arithmetic and copies ran while one was open for 4% of the time, Pallas kernels for 0%

profile of v1, /device:TPU:1, one launch (start us, length us, event | category | flops | bytes accessed | tf_op | source)
XLA Modules:
  0.0 146.2 jit_solution(1520557412052267432)
XLA Ops:
  2.7 1.3 reshape.794
  4.0 11.6 %all-to-all-start = ((f32[16,1,1280]{2,1,0:T(1,128)}), f32[16,1,1280]{2,1,0:T(1,128)S(1)}, u32[]{:S(2)}, u32[]{:S(2)}) async-start(f32[16,1,1280]{2,1,0:T(1,128)} %reshape.794), calls=%async_computation | async-start | bytes 163840 | tf_op jit(solution)/shard_map/all_to_all | solution.py:115
  15.9 1.4 slice_bitcast_fusion.1
  18.4 6.3 %all-to-all-done = f32[16,1,1280]{2,1,0:T(1,128)S(1)} async-done(((f32[16,1,1280]{2,1,0:T(1,128)}), f32[16,1,1280]{2,1,0:T(1,128)S(1)}, u32[]{:S(2)}, u32[]{:S(2)}) %all-to-all-start) | async-done | bytes 81952 | tf_op jit(solution)/shard_map/all_to_all | solution.py:115
  29.0 7.1 %all-to-all-start.1 = ((f32[16,1,640]{2,1,0:T(1,128)}), f32[16,1,640]{2,1,0:T(1,128)S(1)}, u32[]{:S(2)}, u32[]{:S(2)}) async-start(f32[16,1,640]{2,1,0:T(1,128)} %reshape.796), calls=%async_computation.1 | async-start | bytes 81920 | tf_op jit(solution)/shard_map/all_to_all | solution.py:120
  36.1 5.8 %all-to-all-done.1 = f32[16,1,640]{2,1,0:T(1,128)S(1)} async-done(((f32[16,1,640]{2,1,0:T(1,128)}), f32[16,1,640]{2,1,0:T(1,128)S(1)}, u32[]{:S(2)}, u32[]{:S(2)}) %all-to-all-start.1) | async-done | bytes 40992 | tf_op jit(solution)/shard_map/all_to_all | solution.py:120
  44.0 1.3 fusion.77
  45.4 1.3 fusion.75
  46.7 1.3 fusion.78
  48.0 1.3 fusion.76
  50.9 3.7 %all-to-all-start.2 = ((f32[16,1,640]{2,1,0:T(1,128)}), f32[16,1,640]{2,1,0:T(1,128)S(1)}, u32[]{:S(2)}, u32[]{:S(2)}) async-start(f32[16,1,640]{2,1,0:T(1,128)} %reshape.798), calls=%async_computation.2 | async-start | bytes 81920 | tf_op jit(solution)/shard_map/all_to_all | solution.py:127
  54.6 5.8 %all-to-all-done.2 = f32[16,1,640]{2,1,0:T(1,128)S(1)} async-done(((f32[16,1,640]{2,1,0:T(1,128)}), f32[16,1,640]{2,1,0:T(1,128)S(1)}, u32[]{:S(2)}, u32[]{:S(2)}) %all-to-all-start.2) | async-done | bytes 40992 | tf_op jit(solution)/shard_map/all_to_all | solution.py:127
  62.8 1.3 reshape.800
  64.2 3.5 %all-to-all-start.3 = ((f32[16,1,1280]{2,1,0:T(1,128)}), f32[16,1,1280]{2,1,0:T(1,128)S(1)}, u32[]{:S(2)}, u32[]{:S(2)}) async-start(f32[16,1,1280]{2,1,0:T(1,128)} %reshape.800), calls=%async_computation.3 | async-start | bytes 163840 | tf_op jit(solution)/shard_map/all_to_all | solution.py:128
  67.9 9.4 %all-to-all-done.3 = f32[16,1,1280]{2,1,0:T(1,128)S(1)} async-done(((f32[16,1,1280]{2,1,0:T(1,128)}), f32[16,1,1280]{2,1,0:T(1,128)S(1)}, u32[]{:S(2)}, u32[]{:S(2)}) %all-to-all-start.3) | async-done | bytes 81952 | tf_op jit(solution)/shard_map/all_to_all | solution.py:128
  79.6 1.4 fusion.8
  82.3 11.8 %all_to_all.114 = f32[16,1,1280]{2,1,0:T(1,128)S(1)} all-to-all(f32[16,1,1280]{2,1,0:T(1,128)S(1)} %reshape.802), channel_id=1, replica_groups=mesh['gx'=16,'gy'=16] {'gx'}, dimensions={0} | all-to-all | bytes 163840 | tf_op jit(solution)/shard_map/all_to_all | solution.py:115
  97.8 5.5 %all-to-all-start.5 = ((f32[16,1,640]{2,1,0:T(1,128)}), f32[16,1,640]{2,1,0:T(1,128)S(1)}, u32[]{:S(2)}, u32[]{:S(2)}) async-start(f32[16,1,640]{2,1,0:T(1,128)} %reshape.804), calls=%async_computation.5 | async-start | bytes 81920 | tf_op jit(solution)/shard_map/all_to_all | solution.py:120
  103.6 5.7 %all-to-all-done.5 = f32[16,1,640]{2,1,0:T(1,128)S(1)} async-done(((f32[16,1,640]{2,1,0:T(1,128)}), f32[16,1,640]{2,1,0:T(1,128)S(1)}, u32[]{:S(2)}, u32[]{:S(2)}) %all-to-all-start.5) | async-done | bytes 40992 | tf_op jit(solution)/shard_map/all_to_all | solution.py:120
  115.7 3.7 %all-to-all-start.6 = ((f32[16,1,640]{2,1,0:T(1,128)}), f32[16,1,640]{2,1,0:T(1,128)S(1)}, u32[]{:S(2)}, u32[]{:S(2)}) async-start(f32[16,1,640]{2,1,0:T(1,128)} %reshape.806), calls=%async_computation.6 | async-start | bytes 81920 | tf_op jit(solution)/shard_map/all_to_all | solution.py:127
  120.3 4.9 %all-to-all-done.6 = f32[16,1,640]{2,1,0:T(1,128)S(1)} async-done(((f32[16,1,640]{2,1,0:T(1,128)}), f32[16,1,640]{2,1,0:T(1,128)S(1)}, u32[]{:S(2)}, u32[]{:S(2)}) %all-to-all-start.6) | async-done | bytes 40992 | tf_op jit(solution)/shard_map/all_to_all | solution.py:127
  127.6 1.3 reshape.808
  128.9 3.5 %all-to-all-start.7 = ((f32[16,1,1280]{2,1,0:T(1,128)}), f32[16,1,1280]{2,1,0:T(1,128)S(1)}, u32[]{:S(2)}, u32[]{:S(2)}) async-start(f32[16,1,1280]{2,1,0:T(1,128)} %reshape.808), calls=%async_computation.7 | async-start | bytes 163840 | tf_op jit(solution)/shard_map/all_to_all | solution.py:128
  134.0 8.0 %all-to-all-done.7 = f32[16,1,1280]{2,1,0:T(1,128)S(1)} async-done(((f32[16,1,1280]{2,1,0:T(1,128)}), f32[16,1,1280]{2,1,0:T(1,128)S(1)}, u32[]{:S(2)}, u32[]{:S(2)}) %all-to-all-start.7) | async-done | bytes 81952 | tf_op jit(solution)/shard_map/all_to_all | solution.py:128
  (119 shorter events, 36.5 us)
Async XLA Ops:
  0.6 67.0 %copy-start = (bf16[20,20]{1,0:T(8,128)(2,1)S(1)}, bf16[20,20]{1,0:T(8,128)(2,1)}, u32[]{:S(2)}) copy-start(bf16[20,20]{1,0:T(8,128)(2,1)} %param.8) | copy-start | bytes 2404
  0.7 1.4 copy-start.1
  4.0 20.7 %all-to-all-start = ((f32[16,1,1280]{2,1,0:T(1,128)}), f32[16,1,1280]{2,1,0:T(1,128)S(1)}, u32[]{:S(2)}, u32[]{:S(2)}) async-start(f32[16,1,1280]{2,1,0:T(1,128)} %reshape.794), calls=%async_computation | async-start | bytes 163840 | tf_op jit(solution)/shard_map/all_to_all | solution.py:115
  17.3 10.2 %copy-start.6 = (f32[1,2,32,16]{2,3,0,1:T(8,128)}, f32[1,2,32,16]{2,3,0,1:T(8,128)S(1)}, u32[]{:S(2)}) copy-start(f32[1,2,32,16]{2,3,0,1:T(8,128)S(1)} %get-tuple-element.34) | copy-start | bytes 12292
  17.3 10.2 %copy-start.8 = (f32[1,2,32,16]{2,3,0,1:T(8,128)}, f32[1,2,32,16]{2,3,0,1:T(8,128)S(1)}, u32[]{:S(2)}) copy-start(f32[1,2,32,16]{2,3,0,1:T(8,128)S(1)} %get-tuple-element.35) | copy-start | bytes 12292
  17.4 25.7 %copy-start.2 = (f32[1,2,64,16]{2,3,0,1:T(8,128)}, f32[1,2,64,16]{2,3,0,1:T(8,128)S(1)}, u32[]{:S(2)}) copy-start(f32[1,2,64,16]{2,3,0,1:T(8,128)S(1)} %get-tuple-element.32) | copy-start | bytes 24580
  17.4 25.7 %copy-start.4 = (f32[1,2,64,16]{2,3,0,1:T(8,128)}, f32[1,2,64,16]{2,3,0,1:T(8,128)S(1)}, u32[]{:S(2)}) copy-start(f32[1,2,64,16]{2,3,0,1:T(8,128)S(1)} %get-tuple-element.33) | copy-start | bytes 24580
  29.0 12.9 %all-to-all-start.1 = ((f32[16,1,640]{2,1,0:T(1,128)}), f32[16,1,640]{2,1,0:T(1,128)S(1)}, u32[]{:S(2)}, u32[]{:S(2)}) async-start(f32[16,1,640]{2,1,0:T(1,128)} %reshape.796), calls=%async_computation.1 | async-start | bytes 81920 | tf_op jit(solution)/shard_map/all_to_all | solution.py:120
  50.9 9.6 %all-to-all-start.2 = ((f32[16,1,640]{2,1,0:T(1,128)}), f32[16,1,640]{2,1,0:T(1,128)S(1)}, u32[]{:S(2)}, u32[]{:S(2)}) async-start(f32[16,1,640]{2,1,0:T(1,128)} %reshape.798), calls=%async_computation.2 | async-start | bytes 81920 | tf_op jit(solution)/shard_map/all_to_all | solution.py:127
  54.6 7.0 %copy-start.10 = (f32[1,2,32,16]{2,3,1,0:T(8,128)}, f32[1,2,32,16]{2,3,1,0:T(8,128)S(1)}, u32[]{:S(2)}) copy-start(f32[1,2,32,16]{2,3,1,0:T(8,128)S(1)} %get-tuple-element.28) | copy-start | bytes 12292
  54.6 7.0 %copy-start.12 = (f32[1,2,32,16]{2,3,1,0:T(8,128)}, f32[1,2,32,16]{2,3,1,0:T(8,128)S(1)}, u32[]{:S(2)}) copy-start(f32[1,2,32,16]{2,3,1,0:T(8,128)S(1)} %get-tuple-element.29) | copy-start | bytes 12292
  64.2 13.2 %all-to-all-start.3 = ((f32[16,1,1280]{2,1,0:T(1,128)}), f32[16,1,1280]{2,1,0:T(1,128)S(1)}, u32[]{:S(2)}, u32[]{:S(2)}) async-start(f32[16,1,1280]{2,1,0:T(1,128)} %reshape.800), calls=%async_computation.3 | async-start | bytes 163840 | tf_op jit(solution)/shard_map/all_to_all | solution.py:128
  78.2 1.4 copy-start.16
  78.2 1.4 copy-start.17
  94.9 1.4 copy-start.7
  95.9 7.5 %copy-start.15 = (f32[4,20,16]{1,2,0:T(8,128)S(1)}, f32[4,20,16]{1,2,0:T(8,128)}, u32[]{:S(2)}) copy-start(f32[4,20,16]{1,2,0:T(8,128)} %get-tuple-element.21) | copy-start | bytes 15364
  95.9 7.6 %copy-start.14 = (f32[4,20,16]{1,2,0:T(8,128)S(1)}, f32[4,20,16]{1,2,0:T(8,128)}, u32[]{:S(2)}) copy-start(f32[4,20,16]{1,2,0:T(8,128)} %get-tuple-element.20) | copy-start | bytes 15364
  96.3 14.1 %copy-start.3 = (f32[1,2,64,16]{2,3,0,1:T(8,128)S(1)}, f32[1,2,64,16]{2,3,0,1:T(8,128)}, u32[]{:S(2)}) copy-start(f32[1,2,64,16]{2,3,0,1:T(8,128)} %copy-done.2) | copy-start | bytes 24580
  96.3 14.1 %copy-start.5 = (f32[1,2,64,16]{2,3,0,1:T(8,128)S(1)}, f32[1,2,64,16]{2,3,0,1:T(8,128)}, u32[]{:S(2)}) copy-start(f32[1,2,64,16]{2,3,0,1:T(8,128)} %copy-done.4) | copy-start | bytes 24580
  97.8 11.4 %all-to-all-start.5 = ((f32[16,1,640]{2,1,0:T(1,128)}), f32[16,1,640]{2,1,0:T(1,128)S(1)}, u32[]{:S(2)}, u32[]{:S(2)}) async-start(f32[16,1,640]{2,1,0:T(1,128)} %reshape.804), calls=%async_computation.5 | async-start | bytes 81920 | tf_op jit(solution)/shard_map/all_to_all | solution.py:120
  114.2 12.2 %copy-start.11 = (f32[1,2,32,16]{2,3,1,0:T(8,128)S(1)}, f32[1,2,32,16]{2,3,1,0:T(8,128)}, u32[]{:S(2)}) copy-start(f32[1,2,32,16]{2,3,1,0:T(8,128)} %copy-done.10) | copy-start | bytes 12292
  114.2 12.2 %copy-start.13 = (f32[1,2,32,16]{2,3,1,0:T(8,128)S(1)}, f32[1,2,32,16]{2,3,1,0:T(8,128)}, u32[]{:S(2)}) copy-start(f32[1,2,32,16]{2,3,1,0:T(8,128)} %copy-done.12) | copy-start | bytes 12292
  115.7 9.6 %all-to-all-start.6 = ((f32[16,1,640]{2,1,0:T(1,128)}), f32[16,1,640]{2,1,0:T(1,128)S(1)}, u32[]{:S(2)}, u32[]{:S(2)}) async-start(f32[16,1,640]{2,1,0:T(1,128)} %reshape.806), calls=%async_computation.6 | async-start | bytes 81920 | tf_op jit(solution)/shard_map/all_to_all | solution.py:127
  128.9 13.2 %all-to-all-start.7 = ((f32[16,1,1280]{2,1,0:T(1,128)}), f32[16,1,1280]{2,1,0:T(1,128)S(1)}, u32[]{:S(2)}, u32[]{:S(2)}) async-start(f32[16,1,1280]{2,1,0:T(1,128)} %reshape.808), calls=%async_computation.7 | async-start | bytes 163840 | tf_op jit(solution)/shard_map/all_to_all | solution.py:128
  (1 other events, 1.4 us)

commit v2 on v1

v2 whole, which is shorter than its diff:
```python
import math

import jax
import jax.numpy as jnp
import numpy as np
from jax import lax
from jax.experimental import pallas as pl
from jax.experimental.pallas import tpu as pltpu
from jax.sharding import PartitionSpec as P

W = 20
WP = 32
GX = 16
GY = 16
Q = 512
F32 = jnp.float32
BF16 = jnp.bfloat16
HIGHEST = lax.Precision.HIGHEST


def frequencies():
    j = np.arange(16)
    return np.where(j < 8, j, j - 16)


def rotation_blocks(length, sign):
    phase = np.mod(frequencies()[:, None] * np.arange(length)[None, :], length)
    angle = sign * 2.0 * np.pi * phase / length
    c, s = np.cos(angle) / np.sqrt(length), np.sin(angle) / np.sqrt(length)
    return np.stack([np.stack([c, -s]), np.stack([s, c])])


def tables():
    eye = np.eye(4)
    fx = rotation_blocks(32, -1.0).reshape(2, 2, 16, 16, 2)
    tx = np.einsum("rskcx,yv->krycsxv", fx, eye).reshape(128, 256)
    fy = rotation_blocks(64, -1.0).reshape(2, 2, 16, 16, 4)
    ty = np.einsum("rskpy->rkpsy", fy).reshape(32, 128)
    iy = rotation_blocks(64, 1.0).reshape(2, 2, 16, 16, 4)
    tyi = np.einsum("rskpy->prysk", iy).reshape(128, 32)
    ix = rotation_blocks(32, 1.0).reshape(2, 2, 16, 16, 2)
    txi = np.einsum("rskcx,yv->crxyksv", ix, eye).reshape(256, 128)
    z, t = np.arange(32), np.arange(16)
    f = frequencies()
    phase = (
        f[None, :, None, None] * z[None, None, :, None] * 16
        + np.arange(4)[:, None, None, None] * t[None, None, None, :] * 32
    )
    angle = np.mod(phase, 512).reshape(4, 16, 512) * (2.0 * np.pi / 512)
    zt = np.stack([np.cos(angle), -np.sin(angle)], axis=1).reshape(128, 512) / np.sqrt(512)
    return [a.astype(np.float32) for a in (tx, ty, tyi, txi, zt)]


def lane_blocks(rows):
    return lax.broadcasted_iota(jnp.int32, (rows, 128), 1) // WP


def block_transpose(parts):
    which = lane_blocks(parts[0].shape[0])
    out = []
    for b in range(4):
        acc = None
        for a in range(4):
            shift = ((a - b) * WP) % 128
            piece = parts[a] if shift == 0 else pltpu.roll(parts[a], shift, 1)
            acc = piece if acc is None else jnp.where(which == a, piece, acc)
        out.append(acc)
    return out


def kernel(
    field, cot, weight, pw, bias, zt_h, tx_h, ty_h, tyi_h, txi_h,
    out_h, gfield_h, gspec_h,
    u, cv, wv, pwv, bv, zt, tx, ty, tyi, txi,
    wt, local, pre, sig, outv, gout, gs, spec,
    s1, s2, s3, s4, e, d, z, v,
    load_sem, store_sem, send_sem, recv_sem,
):
    cx = lax.axis_index("gx")
    cy = lax.axis_index("gy")

    sources = (field, zt_h, tx_h, ty_h, tyi_h, txi_h, weight, pw, bias, cot)
    sinks = (u, zt, tx, ty, tyi, txi, wv, pwv, bv, cv)
    loads = [
        pltpu.make_async_copy(a, b, load_sem.at[i]) for i, (a, b) in enumerate(zip(sources, sinks))
    ]
    for copy in loads:
        copy.start()

    def peer_x(off):
        dx, dz = off // 4, off % 4
        return lax.rem(cx // 4 + dx, 4) * 4 + lax.rem(lax.rem(cx, 4) + dz, 4)

    def peer_y(off):
        dz, rest = off // 8, off % 8
        dy, dc = rest // 2, rest % 2
        zl, yy, cc = cy // 8, lax.rem(cy // 2, 4), lax.rem(cy, 2)
        return lax.rem(zl + dz, 2) * 8 + lax.rem(yy + dy, 4) * 2 + lax.rem(cc + dc, 2)

    def ring(n):
        return min(n, 4 - n)

    order_x = sorted(range(1, 16), key=lambda o: -(ring(o // 4) + 2 * ring(o % 4)))
    order_y = sorted(range(1, 16), key=lambda o: -(3 * (o // 8) + 3 * ring((o % 8) // 2) + o % 2))

    barrier = pltpu.get_barrier_semaphore()
    for off in order_x:
        pl.semaphore_signal(
            barrier, inc=1, device_id=(peer_x(off), cy), device_id_type=pl.DeviceIdType.MESH
        )
    for off in order_y:
        pl.semaphore_signal(
            barrier, inc=1, device_id=(cx, peer_y(off)), device_id_type=pl.DeviceIdType.MESH
        )

    def exchange(step, axis, src, dst):
        copies = []
        for off in order_x if axis == "gx" else order_y:
            if axis == "gx":
                peer, me, device = peer_x(off), cx, (peer_x(off), cy)
            else:
                peer, me, device = peer_y(off), cy, (cx, peer_y(off))
            copy = pltpu.make_async_remote_copy(
                src_ref=src.at[peer],
                dst_ref=dst.at[me],
                send_sem=send_sem.at[step, off],
                recv_sem=recv_sem.at[step, off],
                device_id=device,
                device_id_type=pl.DeviceIdType.MESH,
            )
            copy.start()
            copies.append(copy)
        me = cx if axis == "gx" else cy
        dst[me] = src[me]
        return copies

    def arrive(copies):
        for copy in copies:
            copy.wait_recv()

    def drain(copies):
        for copy in copies:
            copy.wait_send()

    def pack_modes(values, send):
        spectra = lax.dot_general(
            zt[...], values[...], (((1,), (1,)), ((), ())), preferred_element_type=F32
        )
        for half in range(2):
            parts = [
                spectra[jt * 32 : jt * 32 + 32, half * 128 : half * 128 + 128] for jt in range(4)
            ]
            for sub, block in enumerate(block_transpose(parts)):
                for s in range(2):
                    send[:, s * 8 + half * 4 + sub, :] = block[s * 16 : s * 16 + 16]

    def unpack_modes(recv, half):
        parts = [
            jnp.concatenate([recv[:, s * 8 + half * 4 + sub, :] for s in range(2)], axis=0)
            for sub in range(4)
        ]
        stacked = jnp.concatenate(block_transpose(parts), axis=0)
        return stacked.T.astype(BF16)

    def matmul(a, b):
        return lax.dot_general(
            a, b, (((1,), (0,)), ((), ())), precision=HIGHEST, preferred_element_type=F32
        )

    kappa = jnp.where(lax.broadcasted_iota(jnp.int32, (16, 128), 1) < WP, 1.0, 2.0).astype(F32)
    gather_base = lane_blocks(16) * WP

    def spread(value, w):
        return jnp.take_along_axis(value, gather_base + w, axis=1)

    loads[0].wait()
    loads[1].wait()
    pack_modes(u, s1)
    pl.semaphore_wait(barrier, 30)
    c0 = exchange(0, "gx", s1, e.at[0])

    for copy in loads[2:]:
        copy.wait()
    zeros = jnp.zeros((16, WP - W), F32)

    @pl.loop(0, W)
    def _(w):
        for s in range(2):
            pieces = []
            for jt in range(4):
                pieces += [wv[jt, s, w], zeros]
            wt[s, w] = jnp.concatenate(pieces, axis=1)

    for xy in range(8):
        rows = slice(xy * WP, xy * WP + WP)
        local[rows] = (
            jnp.dot(pwv[0], u[rows], preferred_element_type=F32) + bv[...]
        )

    arrive(c0)
    s2[...] = matmul(tx[...], e[0].reshape(256, 128)).reshape(16, 8, 128)
    c1 = exchange(1, "gy", s2, d.at[0])
    arrive(c1)
    spec[...] = matmul(ty[...], d[0].reshape(128, 128))

    def mix(w, acc):
        sr, si = spread(spec[0:16], w), spread(spec[16:32], w)
        wr, wi = wt[0, w], wt[1, w]
        return acc[0] + wr * sr - wi * si, acc[1] + wi * sr + wr * si

    acc = (jnp.zeros((16, 128), F32), jnp.zeros((16, 128), F32))
    for w in range(W):
        acc = mix(w, acc)
    mixed = jnp.concatenate([acc[0] * kappa, acc[1] * kappa], axis=0)

    s3[...] = matmul(tyi[...], mixed).reshape(16, 8, 128)
    c2 = exchange(2, "gy", s3, z.at[0])
    arrive(c2)
    s4[...] = matmul(txi[...], z[0].reshape(128, 128)).reshape(16, 16, 128)
    c3 = exchange(3, "gx", s4, v.at[0])
    drain(c0)
    arrive(c3)

    for half in range(2):
        rows = slice(half * 128, half * 128 + 128)
        pre[rows] = local[rows] + jnp.dot(
            unpack_modes(v.at[0], half), zt[...], preferred_element_type=F32
        )
    root = math.sqrt(2.0 / math.pi)
    for xy in range(8):
        rows = slice(xy * WP, xy * WP + WP)
        p = pre[rows]
        square = p * p
        t = jnp.tanh(root * p * (1.0 + 0.044715 * square))
        outv[rows] = (0.5 * p * (1.0 + t)).astype(BF16)
        slope = 0.5 * (1.0 + t) + (0.5 * root) * p * (1.0 - t * t) * (
            1.0 + (3.0 * 0.044715) * square
        )
        sig[rows] = (cv[rows].astype(F32) * slope).astype(BF16)

    pack_modes(sig, s1)
    c4 = exchange(4, "gx", s1, e.at[1])
    put_out = pltpu.make_async_copy(outv, out_h, store_sem.at[0])
    put_out.start()
    for xy in range(8):
        rows = slice(xy * WP, xy * WP + WP)
        local[rows] = jnp.dot(pwv[1], sig[rows], preferred_element_type=F32)
    drain(c1)
    drain(c2)
    drain(c3)
    arrive(c4)
    s2[...] = matmul(tx[...], e[1].reshape(256, 128)).reshape(16, 8, 128)
    c5 = exchange(5, "gy", s2, d.at[1])
    arrive(c5)
    back = matmul(ty[...], d[1].reshape(128, 128))
    br, bi = back[0:16] * kappa, back[16:32] * kappa

    lane = lax.broadcasted_iota(jnp.int32, (32, 128), 1)

    def combine(a, b, h):
        bit = (lane & h) != 0
        flip = lane ^ h
        if b is None:
            return jnp.where(bit, 0.0, a + jnp.take_along_axis(a, flip, axis=1))
        return jnp.where(bit, b, a) + jnp.take_along_axis(jnp.where(bit, a, b), flip, axis=1)

    def product(w):
        wr, wi = wt[0, w], wt[1, w]
        return jnp.concatenate([wr * br + wi * bi, wr * bi - wi * br], axis=0)

    def reduce_tree(w, h):
        if h == 32:
            return product(w) if w < W else None
        a, b = reduce_tree(w, h * 2), reduce_tree(w + h, h * 2)
        return combine(a, b, h) if a is not None else None

    back_mixed = reduce_tree(0, 1)
    s3[...] = matmul(tyi[...], back_mixed).reshape(16, 8, 128)
    c6 = exchange(6, "gy", s3, z.at[1])

    @pl.loop(0, W)
    def _(w):
        sr, si = spread(spec[0:16], w), spread(spec[16:32], w)
        parts = (sr * br + si * bi, sr * bi - si * br)
        for s in range(2):
            for jt in range(4):
                gs[jt, s, w] = parts[s][:, jt * WP : jt * WP + W]

    put_gs = pltpu.make_async_copy(gs, gspec_h, store_sem.at[1])
    put_gs.start()

    arrive(c6)
    s4[...] = matmul(txi[...], z[1].reshape(128, 128)).reshape(16, 16, 128)
    c7 = exchange(7, "gx", s4, v.at[1])
    drain(c4)
    drain(c5)
    drain(c6)
    arrive(c7)
    for half in range(2):
        rows = slice(half * 128, half * 128 + 128)
        gout[rows] = (
            local[rows]
            + jnp.dot(unpack_modes(v.at[1], half), zt[...], preferred_element_type=F32)
        ).astype(BF16)
    put_grad = pltpu.make_async_copy(gout, gfield_h, store_sem.at[2])
    put_grad.start()
    drain(c7)
    put_out.wait()
    put_gs.wait()
    put_grad.wait()


def on_device(field, cotangent, spectral_weight, pointwise_weight, channel_bias):
    tx, ty, tyi, txi, zt = tables()

    def rows(a):
        a = jnp.transpose(a, (1, 2, 0, 3)).reshape(8, W, Q)
        return jnp.pad(a, ((0, 0), (0, WP - W), (0, 0))).reshape(8 * WP, Q)

    def cells(a):
        a = a.reshape(2, 4, WP, Q)[:, :, :W]
        return jnp.transpose(a, (2, 0, 1, 3))

    pad = ((0, WP - W), (0, WP - W))
    pw = jnp.stack([jnp.pad(pointwise_weight.T, pad), jnp.pad(pointwise_weight, pad)])
    bias = jnp.pad(channel_bias, (0, WP - W)).reshape(WP, 1)
    weight = jnp.transpose(spectral_weight, (0, 1, 2, 4, 5, 3)).reshape(4, 2, W, 16, W)
    any_spec = pl.BlockSpec(memory_space=pl.ANY)
    out, gfield, gspec = pl.pallas_call(
        kernel,
        out_shape=(
            jax.ShapeDtypeStruct((256, Q), BF16),
            jax.ShapeDtypeStruct((256, Q), BF16),
            jax.ShapeDtypeStruct((4, 2, W, 16, W), F32),
        ),
        in_specs=[any_spec] * 10,
        out_specs=(any_spec,) * 3,
        scratch_shapes=[
            pltpu.VMEM((256, Q), BF16),
            pltpu.VMEM((256, Q), BF16),
            pltpu.VMEM((4, 2, W, 16, W), F32),
            pltpu.VMEM((2, WP, WP), BF16),
            pltpu.VMEM((WP, 1), F32),
            pltpu.VMEM((128, Q), BF16),
            pltpu.VMEM((128, 256), F32),
            pltpu.VMEM((32, 128), F32),
            pltpu.VMEM((128, 32), F32),
            pltpu.VMEM((256, 128), F32),
            pltpu.VMEM((2, W, 16, 128), F32),
            pltpu.VMEM((256, Q), F32),
            pltpu.VMEM((256, Q), F32),
            pltpu.VMEM((256, Q), BF16),
            pltpu.VMEM((256, Q), BF16),
            pltpu.VMEM((256, Q), BF16),
            pltpu.VMEM((4, 2, W, 16, W), F32),
            pltpu.VMEM((32, 128), F32),
            pltpu.VMEM((16, 16, 128), F32),
            pltpu.VMEM((16, 8, 128), F32),
            pltpu.VMEM((16, 8, 128), F32),
            pltpu.VMEM((16, 16, 128), F32),
            pltpu.VMEM((2, 16, 16, 128), F32),
            pltpu.VMEM((2, 16, 8, 128), F32),
            pltpu.VMEM((2, 16, 8, 128), F32),
            pltpu.VMEM((2, 16, 16, 128), F32),
            pltpu.SemaphoreType.DMA((10,)),
            pltpu.SemaphoreType.DMA((3,)),
            pltpu.SemaphoreType.DMA((8, 16)),
            pltpu.SemaphoreType.DMA((8, 16)),
        ],
        compiler_params=pltpu.CompilerParams(
            collective_id=0, has_side_effects=True, vmem_limit_bytes=40 << 20
        ),
    )(
        rows(field), rows(cotangent), weight, pw, bias,
        jnp.asarray(zt, BF16), tx, ty, tyi, txi,
    )
    grad = jnp.transpose(gspec.reshape(4, 2, W, 1, 16, W), (0, 1, 2, 5, 3, 4))
    return cells(out), cells(gfield), grad


def solution(mesh):
    return jax.shard_map(
        on_device,
        mesh=mesh,
        in_specs=(
            P(None, "gx", "gy", None),
            P(None, "gx", "gy", None),
            P("gx", None, None, None, "gy", None),
            P(),
            P(),
        ),
        out_specs=(
            P(None, "gx", "gy", None),
            P(None, "gx", "gy", None),
            P("gx", None, None, None, "gy", None),
        ),
        check_vma=False,
    )
```

time: 147 us -> 68.7 us (0.47)
  Pallas kernels: 0 us -> 60 us
  waiting for transfers between devices: 45.9 us -> 0 us
  starting transfers between devices: 38.6 us -> 0 us
  local copies, waits for them, and re-layouts: 23.7 us -> 7.79 us
  matrix products: 15.5 us -> 0 us
  blocking collectives: 11.8 us -> 0 us
  other arithmetic: 9.31 us -> 0.01 us
    pallas_call x0 -> x1, Pallas kernels: none -> 60 us  [on_device(): pl.pallas_call(kernel, out_shape=(jax.ShapeDtypeStruct((256, Q), BF16), j...]
    all_to_all x7 -> x0, waiting for transfers between devices: 45.9 us -> none  [the longest x2 17.4 us: inverse_cells(): lax.all_to_all(partial_inverse(returned), 'gx', split_axis=4, concat_axis...]
    all_to_all x7 -> x0, starting transfers between devices: 38.6 us -> none  [the longest x2 12.6 us: forward_spectrum(): lax.all_to_all(second_section, 'gy', split_axis=3, concat_axis=4, tiled=T...]
    dot_general x22 -> x0, matrix products: 15.5 us -> none  [the longest x4 5.35 us: mix_pair(): jnp.einsum('mwkj,mwokj->mokj', left_part, right_part, precision=HIGHEST_P...]
    all_to_all x1 -> x0, blocking collectives: 11.8 us -> none  [forward_spectrum(): lax.all_to_all(first_section, 'gx', split_axis=0, concat_axis=4, tiled=True)]
    unnamed x54 -> x16, local copies, waits for them, and re-layouts: 14.2 us -> 4.21 us
    all_to_all x8 -> x0, other arithmetic: 6.54 us -> none  [the longest x2 1.73 us: inverse_cells(): lax.all_to_all(partial_inverse(returned), 'gx', split_axis=4, concat_axis...]
    all_to_all x11 -> x0, local copies, waits for them, and re-layouts: 3.13 us -> none  [the longest x5 1.73 us: forward_spectrum(): lax.all_to_all(first_section, 'gx', split_axis=0, concat_axis=4, tiled=True)]
  transfers between devices with their start and end apart: 7 -> 0, of which waited for: 7 -> 0; matrix products, arithmetic and copies ran while one was open for 4% -> 0% of each run, Pallas kernels for 0% -> 0%
where the time goes in v2:
time: 68.7 us; the launch traced here: 68.5 us
  Pallas kernels  60 us (87%)
  local copies, waits for them, and re-layouts  7.79 us (11%)
  between operations  0.76 us (1%)
    pallas_call x1, Pallas kernels, on_device(): pl.pallas_call(kernel, out_shape=(jax.ShapeDtypeStruct((256, Q), BF16), j...  60 us
    unnamed x16, local copies, waits for them, and re-layouts  4.21 us
    reshape x2, local copies, waits for them, and re-layouts, rows(): a = jnp.transpose(a, (1, 2, 0, 3)).reshape(8, W, Q)  1.94 us

profile of v2, /device:TPU:1, one launch (start us, length us, event | category | flops | bytes accessed | tf_op | source)
XLA Modules:
  0.0 68.5 jit_solution(12143584712905527044)
XLA Ops:
  0.6 0.0 copy-start.1
  0.6 0.0 copy-start.5
  0.7 0.0 copy-start.2
  0.7 0.0 copy-start.3
  0.7 0.0 copy-start
  0.7 0.8 %pad_bitcast_fusion.2 = f32[32,1]{0,1:T(1,128)S(1)} fusion(f32[20]{0:T(128)} %param.14), kind=kLoop, calls=%fused_computation.5 | loop fusion | bytes 208 | tf_op jit(solution)/shard_map/reshape | solution.py:326
  1.5 0.8 %copy.16 = bf16[20,20]{0,1:T(8,128)(2,1)S(1)} copy(bf16[20,20]{1,0:T(8,128)(2,1)} %param.13) | data formatting | bytes 1600 | tf_op args[3]
  2.3 0.7 %pad_bitcast_fusion = (bf16[1,32,32]{2,1,0:T(8,128)(2,1)S(1)}, bf16[1,32,32]{2,1,0:T(8,128)(2,1)S(1)}) fusion(bf16[20,20]{1,0:T(8,128)(2,1)} %param.13, bf16[20,20]{1,0:T(8,128)(2,1)S(1)} %bitcast.43), kind=kLoop, calls=%fused_computation.3 | loop fusion | bytes 5696 | tf_op jit(solution)/shard_map/stack | solution.py:325
  3.0 0.1 copy.17.bias
  3.1 1.0 %copy.21 = bf16[2,4,20,512]{3,2,1,0:T(8,128)(2,1)S(1)} copy(bf16[2,4,20,512]{3,1,0,2:T(4,128)(2,1)} %bitcast.39) | data formatting | bytes 327680 | tf_op jit(solution)/shard_map/reshape | solution.py:317
  4.1 1.0 %copy.22 = bf16[2,4,20,512]{3,2,1,0:T(8,128)(2,1)S(1)} copy(bf16[2,4,20,512]{3,1,0,2:T(4,128)(2,1)} %bitcast.40) | data formatting | bytes 327680 | tf_op jit(solution)/shard_map/reshape | solution.py:317
  5.1 0.0 copy-done.1
  5.1 0.0 copy-done.5
  5.1 0.0 copy-done.2
  5.1 0.0 copy-done.3
  5.1 0.0 copy-done
  5.1 0.0 copy-start.4
  5.1 0.8 %copy-done.4 = f32[128,32]{1,0:T(8,128)S(1)} copy-done((f32[128,32]{1,0:T(8,128)S(1)}, f32[128,32]{1,0:T(8,128)}, u32[]{:S(2)}) %copy-start.4) | copy-done | bytes 16408
  6.0 60.0 %shard_map.121 = (bf16[256,512]{1,0:T(8,128)(2,1)S(1)}, bf16[256,512]{1,0:T(8,128)(2,1)S(1)}, f32[4,2,20,16,20]{4,3,2,1,0:T(8,128)S(1)}) custom-call(bf16[256,512]{1,0:T(8,128)(2,1)S(1)} %bitcast.33, bf16[256,512]{1,0:T(8,128)(2,1)S(1)} %bitcast.34, f32[4,2,20,16,20]{4,3,2,1,0:T(8,128)S(1)} %bitcast.31, bf16[2,32,32]{2,1,0:T(8,128)(2,1)S(1)} %pad_maximum_fusion.pw, ...), custom_call_target="tpu_custom_call" | custom-call | tf_op jit(solution)/shard_map/pallas_call | solution.py:329
  65.9 0.8 %copy.28 = bf16[2,4,20,512]{3,1,0,2:T(4,128)(2,1)} copy(bf16[2,4,20,512]{3,2,1,0:T(8,128)(2,1)S(1)} %slice.8) | data formatting | bytes 327680
  66.7 0.8 %copy.27 = bf16[2,4,20,512]{3,1,0,2:T(4,128)(2,1)} copy(bf16[2,4,20,512]{3,2,1,0:T(8,128)(2,1)S(1)} %slice.9) | data formatting | bytes 327680
  67.5 1.1 %copy.30 = f32[4,2,20,20,1,16]{3,5,4,2,1,0:T(8,128)} copy(f32[4,2,20,20,1,16]{3,5,4,2,1,0:T(8,128)S(1)} %bitcast.32) | data formatting | bytes 409600
  (5 shorter events, 0.1 us)
Async XLA Ops:
  0.6 4.4 %copy-start.1 = (f32[256,128]{1,0:T(8,128)S(1)}, f32[256,128]{1,0:T(8,128)}, u32[]{:S(2)}) copy-start(f32[256,128]{1,0:T(8,128)} %constant.19.clone.txi_h) | copy-start | bytes 393220
  0.6 4.4 %copy-start.5 = (f32[32,128]{1,0:T(8,128)S(1)}, f32[32,128]{1,0:T(8,128)}, u32[]{:S(2)}) copy-start(f32[32,128]{1,0:T(8,128)} %constant.17.clone.ty_h) | copy-start | bytes 49156
  0.7 4.4 %copy-start.2 = (f32[128,256]{1,0:T(8,128)S(1)}, f32[128,256]{1,0:T(8,128)}, u32[]{:S(2)}) copy-start(f32[128,256]{1,0:T(8,128)} %constant.16.clone.tx_h) | copy-start | bytes 393220
  0.7 4.4 %copy-start.3 = (bf16[128,512]{1,0:T(8,128)(2,1)S(1)}, bf16[128,512]{1,0:T(8,128)(2,1)}, u32[]{:S(2)}) copy-start(bf16[128,512]{1,0:T(8,128)(2,1)} %constant.15.clone.zt_h) | copy-start | bytes 393220
  0.7 4.4 %copy-start = (f32[4,2,20,20,1,16]{3,5,4,2,1,0:T(8,128)S(1)}, f32[4,2,20,20,1,16]{3,5,4,2,1,0:T(8,128)}, u32[]{:S(2)}) copy-start(f32[4,2,20,20,1,16]{3,5,4,2,1,0:T(8,128)} %param.12) | copy-start | bytes 614404
  5.1 0.8 %copy-start.4 = (f32[128,32]{1,0:T(8,128)S(1)}, f32[128,32]{1,0:T(8,128)}, u32[]{:S(2)}) copy-start(f32[128,32]{1,0:T(8,128)} %constant.18.clone.tyi_h) | copy-start | bytes 49156

commit v3 on v2

--- a/solution.py
+++ b/solution.py
@@ -30,16 +30,22 @@
     return np.stack([np.stack([c, -s]), np.stack([s, c])])
 
 
+def split(a):
+    a = a.astype(np.float32)
+    hi = a.astype(BF16)
+    lo = (a - hi.astype(np.float32)).astype(BF16)
+    return np.concatenate([hi, lo, hi], axis=1)
+
+
 def tables():
-    eye = np.eye(4)
     fx = rotation_blocks(32, -1.0).reshape(2, 2, 16, 16, 2)
-    tx = np.einsum("rskcx,yv->krycsxv", fx, eye).reshape(128, 256)
+    tx = np.einsum("rskcx->krcsx", fx).reshape(32, 64)
     fy = rotation_blocks(64, -1.0).reshape(2, 2, 16, 16, 4)
     ty = np.einsum("rskpy->rkpsy", fy).reshape(32, 128)
     iy = rotation_blocks(64, 1.0).reshape(2, 2, 16, 16, 4)
     tyi = np.einsum("rskpy->prysk", iy).reshape(128, 32)
     ix = rotation_blocks(32, 1.0).reshape(2, 2, 16, 16, 2)
-    txi = np.einsum("rskcx,yv->crxyksv", ix, eye).reshape(256, 128)
+    txi = np.einsum("rskcx->crxks", ix).reshape(64, 32)
     z, t = np.arange(32), np.arange(16)
     f = frequencies()
     phase = (
@@ -48,7 +54,7 @@
     )
     angle = np.mod(phase, 512).reshape(4, 16, 512) * (2.0 * np.pi / 512)
     zt = np.stack([np.cos(angle), -np.sin(angle)], axis=1).reshape(128, 512) / np.sqrt(512)
-    return [a.astype(np.float32) for a in (tx, ty, tyi, txi, zt)]
+    return [zt.astype(np.float32).astype(BF16)] + [split(a) for a in (tx, ty, tyi, txi)]
 
 
 def lane_blocks(rows):
@@ -71,8 +77,8 @@
 def kernel(
     field, cot, weight, pw, bias, zt_h, tx_h, ty_h, tyi_h, txi_h,
     out_h, gfield_h, gspec_h,
-    u, cv, wv, pwv, bv, zt, tx, ty, tyi, txi,
-    wt, local, pre, sig, outv, gout, gs, spec,
+    fin, cin, wv, pwv, bv, zt, tx, ty, tyi, txi,
+    u, cells, ccells, square, wt, local, pre, sig, outv, gout, gs, spec,
     s1, s2, s3, s4, e, d, z, v,
     load_sem, store_sem, send_sem, recv_sem,
 ):
@@ -80,7 +86,7 @@
     cy = lax.axis_index("gy")
 
     sources = (field, zt_h, tx_h, ty_h, tyi_h, txi_h, weight, pw, bias, cot)
-    sinks = (u, zt, tx, ty, tyi, txi, wv, pwv, bv, cv)
+    sinks = (fin, zt, tx, ty, tyi, txi, wv, pwv, bv, cin)
     loads = [
         pltpu.make_async_copy(a, b, load_sem.at[i]) for i, (a, b) in enumerate(zip(sources, sinks))
     ]
@@ -162,10 +168,33 @@
         stacked = jnp.concatenate(block_transpose(parts), axis=0)
         return stacked.T.astype(BF16)
 
-    def matmul(a, b):
-        return lax.dot_general(
-            a, b, (((1,), (0,)), ((), ())), precision=HIGHEST, preferred_element_type=F32
+    def matmul(table, b):
+        hi = b.astype(BF16)
+        lo = (b - hi.astype(F32)).astype(BF16)
+        return jnp.dot(
+            table[...], jnp.concatenate([hi, hi, lo], axis=0), preferred_element_type=F32
         )
+
+    def y_to_lanes(recv, n):
+        return jnp.concatenate([recv[pl.ds(y, n, stride=4), :] for y in range(4)], axis=1)
+
+    def x_forward(recv, send):
+        out = matmul(tx, y_to_lanes(recv, 64))
+        for y in range(4):
+            send[pl.ds(y, 32, stride=4), :] = out[:, y * 128 : y * 128 + 128]
+
+    def x_inverse(recv, send):
+        out = matmul(txi, y_to_lanes(recv, 32))
+        for y in range(4):
+            send[pl.ds(y, 64, stride=4), :] = out[:, y * 128 : y * 128 + 128]
+
+    def to_cells(source, target):
+        for x in range(2):
+            target[:, 4 * x : 4 * x + 4, :] = source[:, x].astype(F32)
+
+    def from_cells(source, target):
+        for x in range(2):
+            target[:, x] = source[:, 4 * x : 4 * x + 4, :].astype(BF16)
 
     kappa = jnp.where(lax.broadcasted_iota(jnp.int32, (16, 128), 1) < WP, 1.0, 2.0).astype(F32)
     gather_base = lane_blocks(16) * WP
@@ -174,6 +203,10 @@
         return jnp.take_along_axis(value, gather_base + w, axis=1)
 
     loads[0].wait()
+    to_cells(fin, cells)
+    pad = jnp.zeros((WP - W, Q), F32)
+    for xy in range(8):
+        u[xy * WP : xy * WP + WP] = jnp.concatenate([cells[:, xy, :], pad], axis=0).astype(BF16)
     loads[1].wait()
     pack_modes(u, s1)
     pl.semaphore_wait(barrier, 30)
@@ -191,68 +224,75 @@
                 pieces += [wv[jt, s, w], zeros]
             wt[s, w] = jnp.concatenate(pieces, axis=1)
 
+    square[...] = jnp.zeros((128, 128), F32)
+    square[0:W, 0:W] = pwv[...].astype(F32)
+    square[WP : WP + 1, 0:W] = bv[...].reshape(1, W)
+    turned = square[...].T
+    pw_back = square[0:WP, 0:WP].astype(BF16)
+    pw_forward = turned[0:WP, 0:WP].astype(BF16)
+    bias_column = turned[0:W, WP : WP + 1]
     for xy in range(8):
         rows = slice(xy * WP, xy * WP + WP)
-        local[rows] = (
-            jnp.dot(pwv[0], u[rows], preferred_element_type=F32) + bv[...]
-        )
+        local[xy] = jnp.dot(pw_forward, u[rows], preferred_element_type=F32)[0:W] + bias_column
+    to_cells(cin, ccells)
 
     arrive(c0)
-    s2[...] = matmul(tx[...], e[0].reshape(256, 128)).reshape(16, 8, 128)
+    x_forward(e.at[0].reshape(256, 128), s2.reshape(128, 128))
     c1 = exchange(1, "gy", s2, d.at[0])
     arrive(c1)
-    spec[...] = matmul(ty[...], d[0].reshape(128, 128))
-
-    def mix(w, acc):
+    spec[...] = matmul(ty, d[0].reshape(128, 128))
+
+    acc_r = acc_i = jnp.zeros((16, 128), F32)
+    for w in range(W):
         sr, si = spread(spec[0:16], w), spread(spec[16:32], w)
         wr, wi = wt[0, w], wt[1, w]
-        return acc[0] + wr * sr - wi * si, acc[1] + wi * sr + wr * si
-
-    acc = (jnp.zeros((16, 128), F32), jnp.zeros((16, 128), F32))
-    for w in range(W):
-        acc = mix(w, acc)
-    mixed = jnp.concatenate([acc[0] * kappa, acc[1] * kappa], axis=0)
-
-    s3[...] = matmul(tyi[...], mixed).reshape(16, 8, 128)
+        acc_r = acc_r + (wr * sr - wi * si)
+        acc_i = acc_i + (wi * sr + wr * si)
+    mixed = jnp.concatenate([acc_r * kappa, acc_i * kappa], axis=0)
+
+    s3[...] = matmul(tyi, mixed).reshape(16, 8, 128)
     c2 = exchange(2, "gy", s3, z.at[0])
     arrive(c2)
-    s4[...] = matmul(txi[...], z[0].reshape(128, 128)).reshape(16, 16, 128)
+    x_inverse(z.at[0].reshape(128, 128), s4.reshape(256, 128))
     c3 = exchange(3, "gx", s4, v.at[0])
     drain(c0)
     arrive(c3)
 
+    root = math.sqrt(2.0 / math.pi)
+    cubic = 0.044715
     for half in range(2):
-        rows = slice(half * 128, half * 128 + 128)
-        pre[rows] = local[rows] + jnp.dot(
-            unpack_modes(v.at[0], half), zt[...], preferred_element_type=F32
-        )
-    root = math.sqrt(2.0 / math.pi)
-    for xy in range(8):
-        rows = slice(xy * WP, xy * WP + WP)
-        p = pre[rows]
-        square = p * p
-        t = jnp.tanh(root * p * (1.0 + 0.044715 * square))
-        outv[rows] = (0.5 * p * (1.0 + t)).astype(BF16)
-        slope = 0.5 * (1.0 + t) + (0.5 * root) * p * (1.0 - t * t) * (
-            1.0 + (3.0 * 0.044715) * square
-        )
-        sig[rows] = (cv[rows].astype(F32) * slope).astype(BF16)
+        spatial = jnp.dot(unpack_modes(v.at[0], half), zt[...], preferred_element_type=F32)
+        for sub in range(4):
+            xy = half * 4 + sub
+            p = local[xy] + spatial[sub * WP : sub * WP + W]
+            pre[xy] = p
+            p2 = p * p
+            t = jnp.tanh(p * (root * cubic * p2 + root))
+            b = p * (1.5 * root * cubic * p2 + 0.5 * root)
+            slope = t * (0.5 - b * t) + (b + 0.5)
+            signal = ccells[:, xy, :] * slope
+            sig[xy * WP : xy * WP + WP] = jnp.concatenate([signal, pad], axis=0).astype(BF16)
 
     pack_modes(sig, s1)
     c4 = exchange(4, "gx", s1, e.at[1])
+
+    for xy in range(8):
+        p = pre[xy]
+        t = jnp.tanh(p * (root * cubic * (p * p) + root))
+        cells[:, xy, :] = 0.5 * p * (1.0 + t)
+        rows = slice(xy * WP, xy * WP + WP)
+        local[xy] = jnp.dot(pw_back, sig[rows], preferred_element_type=F32)[0:W]
+    from_cells(cells, outv)
     put_out = pltpu.make_async_copy(outv, out_h, store_sem.at[0])
     put_out.start()
-    for xy in range(8):
-        rows = slice(xy * WP, xy * WP + WP)
-        local[rows] = jnp.dot(pwv[1], sig[rows], preferred_element_type=F32)
     drain(c1)
     drain(c2)
     drain(c3)
     arrive(c4)
-    s2[...] = matmul(tx[...], e[1].reshape(256, 128)).reshape(16, 8, 128)
+    x_forward(e.at[1].reshape(256, 128), s2.reshape(128, 128))
     c5 = exchange(5, "gy", s2, d.at[1])
     arrive(c5)
-    back = matmul(ty[...], d[1].reshape(128, 128))
+    back = matmul(ty, d[1].reshape(128, 128))
     br, bi = back[0:16] * kappa, back[16:32] * kappa
 
     lane = lax.broadcasted_iota(jnp.int32, (32, 128), 1)
@@ -269,13 +309,12 @@
         return jnp.concatenate([wr * br + wi * bi, wr * bi - wi * br], axis=0)
 
     def reduce_tree(w, h):
-        if h == 32:
+        if h == WP:
             return product(w) if w < W else None
         a, b = reduce_tree(w, h * 2), reduce_tree(w + h, h * 2)
         return combine(a, b, h) if a is not None else None
 
-    back_mixed = reduce_tree(0, 1)
-    s3[...] = matmul(tyi[...], back_mixed).reshape(16, 8, 128)
+    s3[...] = matmul(tyi, reduce_tree(0, 1)).reshape(16, 8, 128)
     c6 = exchange(6, "gy", s3, z.at[1])
 
     @pl.loop(0, W)
@@ -290,18 +329,18 @@
     put_gs.start()
 
     arrive(c6)
-    s4[...] = matmul(txi[...], z[1].reshape(128, 128)).reshape(16, 16, 128)
+    x_inverse(z.at[1].reshape(128, 128), s4.reshape(256, 128))
     c7 = exchange(7, "gx", s4, v.at[1])
     drain(c4)
     drain(c5)
     drain(c6)
     arrive(c7)
     for half in range(2):
-        rows = slice(half * 128, half * 128 + 128)
-        gout[rows] = (
-            local[rows]
-            + jnp.dot(unpack_modes(v.at[1], half), zt[...], preferred_element_type=F32)
-        ).astype(BF16)
+        spatial = jnp.dot(unpack_modes(v.at[1], half), zt[...], preferred_element_type=F32)
+        for sub in range(4):
+            xy = half * 4 + sub
+            cells[:, xy, :] = local[xy] + spatial[sub * WP : sub * WP + W]
+    from_cells(cells, gout)
     put_grad = pltpu.make_async_copy(gout, gfield_h, store_sem.at[2])
     put_grad.start()
     drain(c7)
@@ -311,47 +350,39 @@
 
 
 def on_device(field, cotangent, spectral_weight, pointwise_weight, channel_bias):
-    tx, ty, tyi, txi, zt = tables()
-
-    def rows(a):
-        a = jnp.transpose(a, (1, 2, 0, 3)).reshape(8, W, Q)
-        return jnp.pad(a, ((0, 0), (0, WP - W), (0, 0))).reshape(8 * WP, Q)
-
-    def cells(a):
-        a = a.reshape(2, 4, WP, Q)[:, :, :W]
-        return jnp.transpose(a, (2, 0, 1, 3))
-
-    pad = ((0, WP - W), (0, WP - W))
-    pw = jnp.stack([jnp.pad(pointwise_weight.T, pad), jnp.pad(pointwise_weight, pad)])
-    bias = jnp.pad(channel_bias, (0, WP - W)).reshape(WP, 1)
+    constants = tables()
     weight = jnp.transpose(spectral_weight, (0, 1, 2, 4, 5, 3)).reshape(4, 2, W, 16, W)
-    any_spec = pl.BlockSpec(memory_space=pl.ANY)
+    hbm = pl.BlockSpec(memory_space=pltpu.MemorySpace.HBM)
     out, gfield, gspec = pl.pallas_call(
         kernel,
         out_shape=(
-            jax.ShapeDtypeStruct((256, Q), BF16),
-            jax.ShapeDtypeStruct((256, Q), BF16),
+            jax.ShapeDtypeStruct((W, 2, 4, Q), BF16),
+            jax.ShapeDtypeStruct((W, 2, 4, Q), BF16),
             jax.ShapeDtypeStruct((4, 2, W, 16, W), F32),
         ),
-        in_specs=[any_spec] * 10,
-        out_specs=(any_spec,) * 3,
+        in_specs=[hbm] * 10,
+        out_specs=(hbm,) * 3,
         scratch_shapes=[
+            pltpu.VMEM((W, 2, 4, Q), BF16),
+            pltpu.VMEM((W, 2, 4, Q), BF16),
+            pltpu.VMEM((4, 2, W, 16, W), F32),
+            pltpu.VMEM((W, W), BF16),
+            pltpu.VMEM((W,), F32),
+            pltpu.VMEM((128, Q), BF16),
+            pltpu.VMEM((32, 192), BF16),
+            pltpu.VMEM((32, 384), BF16),
+            pltpu.VMEM((128, 96), BF16),
+            pltpu.VMEM((64, 96), BF16),
             pltpu.VMEM((256, Q), BF16),
+            pltpu.VMEM((W, 8, Q), F32),
+            pltpu.VMEM((W, 8, Q), F32),
+            pltpu.VMEM((128, 128), F32),
+            pltpu.VMEM((2, W, 16, 128), F32),
+            pltpu.VMEM((8, W, Q), F32),
+            pltpu.VMEM((8, W, Q), F32),
             pltpu.VMEM((256, Q), BF16),
-            pltpu.VMEM((4, 2, W, 16, W), F32),
-            pltpu.VMEM((2, WP, WP), BF16),
-            pltpu.VMEM((WP, 1), F32),
-            pltpu.VMEM((128, Q), BF16),
-            pltpu.VMEM((128, 256), F32),
-            pltpu.VMEM((32, 128), F32),
-            pltpu.VMEM((128, 32), F32),
-            pltpu.VMEM((256, 128), F32),
-            pltpu.VMEM((2, W, 16, 128), F32),
-            pltpu.VMEM((256, Q), F32),
-            pltpu.VMEM((256, Q), F32),
-            pltpu.VMEM((256, Q), BF16),
-            pltpu.VMEM((256, Q), BF16),
-            pltpu.VMEM((256, Q), BF16),
+            pltpu.VMEM((W, 2, 4, Q), BF16),
+            pltpu.VMEM((W, 2, 4, Q), BF16),
             pltpu.VMEM((4, 2, W, 16, W), F32),
             pltpu.VMEM((32, 128), F32),
             pltpu.VMEM((16, 16, 128), F32),
@@ -370,12 +401,9 @@
         compiler_params=pltpu.CompilerParams(
             collective_id=0, has_side_effects=True, vmem_limit_bytes=40 << 20
         ),
-    )(
-        rows(field), rows(cotangent), weight, pw, bias,
-        jnp.asarray(zt, BF16), tx, ty, tyi, txi,
-    )
+    )(field, cotangent, weight, pointwise_weight, channel_bias, *constants)
     grad = jnp.transpose(gspec.reshape(4, 2, W, 1, 16, W), (0, 1, 2, 5, 3, 4))
-    return cells(out), cells(gfield), grad
+    return out, gfield, grad
 
 
 def solution(mesh):

time: 68.7 us -> 69.7 us (1.015)
  local copies, waits for them, and re-layouts: 7.79 us -> 10.7 us
  Pallas kernels: 60 us -> 57.9 us
    unnamed x16 -> x23, local copies, waits for them, and re-layouts: 4.21 us -> 10.7 us
    reshape x4 -> x0, local copies, waits for them, and re-layouts: 2.8 us -> none  [the longest x2 1.94 us: rows(): a = jnp.transpose(a, (1, 2, 0, 3)).reshape(8, W, Q)]
    pallas_call x1, Pallas kernels: 60 us -> 57.9 us  [on_device(): pl.pallas_call(kernel, out_shape=(jax.ShapeDtypeStruct((W, 2, 4, Q), BF16...]
    another operation x1 -> x0, local copies, waits for them, and re-layouts: 0.7 us -> none  [on_device(): jnp.stack([jnp.pad(pointwise_weight.T, pad), jnp.pad(pointwise_weight, pa...]
where the time goes in v3:
time: 69.7 us; the launch traced here: 69.2 us
  Pallas kernels  57.9 us (83%)
  local copies, waits for them, and re-layouts  10.7 us (15%)
    pallas_call x1, Pallas kernels, on_device(): pl.pallas_call(kernel, out_shape=(jax.ShapeDtypeStruct((W, 2, 4, Q), BF16...  57.9 us
    unnamed x23, local copies, waits for them, and re-layouts  10.7 us

profile of v3, /device:TPU:1, one launch (start us, length us, event | category | flops | bytes accessed | tf_op | source)
XLA Modules:
  0.0 69.2 jit_solution(16610936523012410575)
XLA Ops:
  0.6 0.0 copy-start
  0.6 1.3 %copy-done = f32[4,2,20,20,1,16]{3,5,4,2,1,0:T(8,128)S(1)} copy-done((f32[4,2,20,20,1,16]{3,5,4,2,1,0:T(8,128)S(1)}, f32[4,2,20,20,1,16]{3,5,4,2,1,0:T(8,128)}, u32[]{:S(2)}) %copy-start) | copy-done | bytes 204824
  1.9 0.0 copy-start.1
  2.0 0.9 %copy-done.1 = bf16[20,2,4,512]{3,2,1,0:T(4,128)(2,1)S(1)} copy-done((bf16[20,2,4,512]{3,2,1,0:T(4,128)(2,1)S(1)}, bf16[20,2,4,512]{3,2,1,0:T(4,128)(2,1)}, u32[]{:S(2)}) %copy-start.1) | copy-done | bytes 163864
  2.9 0.0 copy-start.2
  2.9 0.9 %copy-done.2 = bf16[20,2,4,512]{3,2,1,0:T(4,128)(2,1)S(1)} copy-done((bf16[20,2,4,512]{3,2,1,0:T(4,128)(2,1)S(1)}, bf16[20,2,4,512]{3,2,1,0:T(4,128)(2,1)}, u32[]{:S(2)}) %copy-start.2) | copy-done | bytes 163864
  3.8 0.0 copy-start.3
  3.8 0.9 %copy-done.3 = bf16[128,512]{1,0:T(8,128)(2,1)S(1)} copy-done((bf16[128,512]{1,0:T(8,128)(2,1)S(1)}, bf16[128,512]{1,0:T(8,128)(2,1)}, u32[]{:S(2)}) %copy-start.3) | copy-done | bytes 131096
  4.7 0.0 copy-start.4
  4.7 0.8 %copy-done.4 = bf16[128,96]{1,0:T(8,128)(2,1)S(1)} copy-done((bf16[128,96]{1,0:T(8,128)(2,1)S(1)}, bf16[128,96]{1,0:T(8,128)(2,1)}, u32[]{:S(2)}) %copy-start.4) | copy-done | bytes 24600
  5.4 0.0 copy-start.5
  5.4 0.7 %copy-done.5 = bf16[32,384]{1,0:T(8,128)(2,1)S(1)} copy-done((bf16[32,384]{1,0:T(8,128)(2,1)S(1)}, bf16[32,384]{1,0:T(8,128)(2,1)}, u32[]{:S(2)}) %copy-start.5) | copy-done | bytes 24600
  6.2 0.0 copy-start.6
  6.2 0.7 %copy-done.6 = bf16[64,96]{1,0:T(8,128)(2,1)S(1)} copy-done((bf16[64,96]{1,0:T(8,128)(2,1)S(1)}, bf16[64,96]{1,0:T(8,128)(2,1)}, u32[]{:S(2)}) %copy-start.6) | copy-done | bytes 12312
  6.9 0.0 copy-start.7
  6.9 0.7 %copy-done.7 = bf16[32,192]{1,0:T(8,128)(2,1)S(1)} copy-done((bf16[32,192]{1,0:T(8,128)(2,1)S(1)}, bf16[32,192]{1,0:T(8,128)(2,1)}, u32[]{:S(2)}) %copy-start.7) | copy-done | bytes 12312
  7.6 0.0 copy-start.8
  7.6 0.7 copy-done.8
  8.3 0.0 copy-start.9
  8.3 0.7 copy-done.9
  9.0 57.9 %shard_map.121 = (bf16[20,2,4,512]{3,2,1,0:T(4,128)(2,1)S(1)}, bf16[20,2,4,512]{3,2,1,0:T(4,128)(2,1)S(1)}, f32[4,2,20,16,20]{4,3,2,1,0:T(8,128)S(1)}) custom-call(bf16[20,2,4,512]{3,2,1,0:T(4,128)(2,1)S(1)} %copy-done.1, bf16[20,2,4,512]{3,2,1,0:T(4,128)(2,1)S(1)} %copy-done.2, f32[4,2,20,16,20]{4,3,2,1,0:T(8,128)S(1)} %bitcast.10, ...), custom_call_target="tpu_custom_call" | custom-call | tf_op jit(solution)/shard_map/pallas_call | solution.py:356
  66.8 0.7 copy.18
  67.5 0.7 copy.19
  68.2 1.1 %copy.20 = f32[4,2,20,20,1,16]{3,5,4,2,1,0:T(8,128)} copy(f32[4,2,20,20,1,16]{3,5,4,2,1,0:T(8,128)S(1)} %bitcast.11) | data formatting | bytes 409600
Async XLA Ops:
  0.6 1.3 %copy-start = (f32[4,2,20,20,1,16]{3,5,4,2,1,0:T(8,128)S(1)}, f32[4,2,20,20,1,16]{3,5,4,2,1,0:T(8,128)}, u32[]{:S(2)}) copy-start(f32[4,2,20,20,1,16]{3,5,4,2,1,0:T(8,128)} %param.12) | copy-start | bytes 614404
  1.9 0.9 %copy-start.1 = (bf16[20,2,4,512]{3,2,1,0:T(4,128)(2,1)S(1)}, bf16[20,2,4,512]{3,2,1,0:T(4,128)(2,1)}, u32[]{:S(2)}) copy-start(bf16[20,2,4,512]{3,2,1,0:T(4,128)(2,1)} %field.1) | copy-start | bytes 491524
  2.9 0.9 %copy-start.2 = (bf16[20,2,4,512]{3,2,1,0:T(4,128)(2,1)S(1)}, bf16[20,2,4,512]{3,2,1,0:T(4,128)(2,1)}, u32[]{:S(2)}) copy-start(bf16[20,2,4,512]{3,2,1,0:T(4,128)(2,1)} %cot.1) | copy-start | bytes 491524
  3.8 0.9 %copy-start.3 = (bf16[128,512]{1,0:T(8,128)(2,1)S(1)}, bf16[128,512]{1,0:T(8,128)(2,1)}, u32[]{:S(2)}) copy-start(bf16[128,512]{1,0:T(8,128)(2,1)} %constant.10.clone.zt_h) | copy-start | bytes 393220
  4.7 0.8 %copy-start.4 = (bf16[128,96]{1,0:T(8,128)(2,1)S(1)}, bf16[128,96]{1,0:T(8,128)(2,1)}, u32[]{:S(2)}) copy-start(bf16[128,96]{1,0:T(8,128)(2,1)} %constant.13.clone.tyi_h) | copy-start | bytes 73732
  5.4 0.7 %copy-start.5 = (bf16[32,384]{1,0:T(8,128)(2,1)S(1)}, bf16[32,384]{1,0:T(8,128)(2,1)}, u32[]{:S(2)}) copy-start(bf16[32,384]{1,0:T(8,128)(2,1)} %constant.12.clone.ty_h) | copy-start | bytes 73732
  6.2 0.7 %copy-start.6 = (bf16[64,96]{1,0:T(8,128)(2,1)S(1)}, bf16[64,96]{1,0:T(8,128)(2,1)}, u32[]{:S(2)}) copy-start(bf16[64,96]{1,0:T(8,128)(2,1)} %constant.14.clone.txi_h) | copy-start | bytes 36868
  6.9 0.7 %copy-start.7 = (bf16[32,192]{1,0:T(8,128)(2,1)S(1)}, bf16[32,192]{1,0:T(8,128)(2,1)}, u32[]{:S(2)}) copy-start(bf16[32,192]{1,0:T(8,128)(2,1)} %constant.11.clone.tx_h) | copy-start | bytes 36868
  7.6 0.7 copy-start.8
  8.3 0.7 copy-start.9

commit v4 on v3

--- a/solution.py
+++ b/solution.py
@@ -399,7 +399,7 @@
             pltpu.SemaphoreType.DMA((8, 16)),
         ],
         compiler_params=pltpu.CompilerParams(
-            collective_id=0, has_side_effects=True, vmem_limit_bytes=40 << 20
+            collective_id=0, has_side_effects=True, vmem_limit_bytes=67043328
         ),
     )(field, cotangent, weight, pointwise_weight, channel_bias, *constants)
     grad = jnp.transpose(gspec.reshape(4, 2, W, 1, 16, W), (0, 1, 2, 5, 3, 4))

time: 69.7 us -> 64.2 us (0.921)
  local copies, waits for them, and re-layouts: 10.7 us -> 5.73 us
    unnamed x23 -> x3, local copies, waits for them, and re-layouts: 10.7 us -> 5.73 us
where the time goes in v4:
time: 64.2 us; the launch traced here: 64 us
  Pallas kernels  57.6 us (90%)
  local copies, waits for them, and re-layouts  5.73 us (9%)
    pallas_call x1, Pallas kernels, on_device(): pl.pallas_call(kernel, out_shape=(jax.ShapeDtypeStruct((W, 2, 4, Q), BF16...  57.6 us
    unnamed x3, local copies, waits for them, and re-layouts  5.73 us

profile of v4, /device:TPU:1, one launch (start us, length us, event | category | flops | bytes accessed | tf_op | source)
XLA Modules:
  0.0 64.0 jit_solution(1264825843700862612)
XLA Ops:
  0.6 57.6 %shard_map.121 = (bf16[20,2,4,512]{3,2,1,0:T(4,128)(2,1)}, bf16[20,2,4,512]{3,2,1,0:T(4,128)(2,1)}, f32[4,2,20,16,20]{4,3,2,1,0:T(8,128)}) custom-call(bf16[20,2,4,512]{3,2,1,0:T(4,128)(2,1)} %field.1, bf16[20,2,4,512]{3,2,1,0:T(4,128)(2,1)} %cot.1, f32[4,2,20,16,20]{4,3,2,1,0:T(8,128)} %bitcast.10, bf16[20,20]{1,0:T(8,128)(2,1)} %pw.1, f32[20]{0:T(128)} %bias.1, ...), custom_call_target="tpu_custom_call" | custom-call | tf_op jit(solution)/shard_map/pallas_call | solution.py:356
  58.3 1.6 %copy.18 = bf16[20,2,4,512]{3,2,1,0:T(4,128)(2,1)} copy(bf16[20,2,4,512]{3,2,1,0:T(4,128)(2,1)} %get-tuple-element.15) | data formatting | bytes 327680
  59.9 1.6 %copy.19 = bf16[20,2,4,512]{3,2,1,0:T(4,128)(2,1)} copy(bf16[20,2,4,512]{3,2,1,0:T(4,128)(2,1)} %get-tuple-element.16) | data formatting | bytes 327680
  61.5 2.5 %copy.20 = f32[4,2,20,20,1,16]{3,5,4,2,1,0:T(8,128)} copy(f32[4,2,20,20,1,16]{3,5,4,2,1,0:T(8,128)} %bitcast.11) | data formatting | bytes 409600

commit v5 on v4

--- a/solution.py
+++ b/solution.py
@@ -15,7 +15,8 @@
 Q = 512
 F32 = jnp.float32
 BF16 = jnp.bfloat16
-HIGHEST = lax.Precision.HIGHEST
+VMEM = 67043328
+RESULTS = 2 * 20 * 8 * 512 * 2 + 160 * 16 * 128 * 4
 
 
 def frequencies():
@@ -76,14 +77,38 @@
 
 def kernel(
     field, cot, weight, pw, bias, zt_h, tx_h, ty_h, tyi_h, txi_h,
-    out_h, gfield_h, gspec_h,
+    outv, gout, gs,
     fin, cin, wv, pwv, bv, zt, tx, ty, tyi, txi,
-    u, cells, ccells, square, wt, local, pre, sig, outv, gout, gs, spec,
+    u, cells, ccells, square, wt, local, pre, sig, spec,
     s1, s2, s3, s4, e, d, z, v,
-    load_sem, store_sem, send_sem, recv_sem,
+    load_sem, send_sem, recv_sem,
 ):
     cx = lax.axis_index("gx")
     cy = lax.axis_index("gy")
+
+    turn_x = [lax.rem(cx // 4 + i, 4) * 4 for i in range(4)]
+    turn_z = [lax.rem(lax.rem(cx, 4) + i, 4) for i in range(4)]
+    turn_l = [lax.rem(cy // 8 + i, 2) * 8 for i in range(2)]
+    turn_y = [lax.rem(cy // 2 + i, 4) * 2 for i in range(4)]
+    turn_c = [lax.rem(cy + i, 2) for i in range(2)]
+    peer_x = [turn_x[o // 4] + turn_z[o % 4] for o in range(16)]
+    peer_y = [turn_l[o // 8] + turn_y[(o % 8) // 2] + turn_c[o % 2] for o in range(16)]
+
+    def ring(n):
+        return min(n, 4 - n)
+
+    order_x = sorted(range(1, 16), key=lambda o: -(ring(o // 4) + 2 * ring(o % 4)))
+    order_y = sorted(range(1, 16), key=lambda o: -(3 * (o // 8) + 3 * ring((o % 8) // 2) + o % 2))
+
+    barrier = pltpu.get_barrier_semaphore()
+    for off in order_x:
+        pl.semaphore_signal(
+            barrier, inc=1, device_id=(peer_x[off], cy), device_id_type=pl.DeviceIdType.MESH
+        )
+    for off in order_y:
+        pl.semaphore_signal(
+            barrier, inc=1, device_id=(cx, peer_y[off]), device_id_type=pl.DeviceIdType.MESH
+        )
 
     sources = (field, zt_h, tx_h, ty_h, tyi_h, txi_h, weight, pw, bias, cot)
     sinks = (fin, zt, tx, ty, tyi, txi, wv, pwv, bv, cin)
@@ -93,39 +118,13 @@
     for copy in loads:
         copy.start()
 
-    def peer_x(off):
-        dx, dz = off // 4, off % 4
-        return lax.rem(cx // 4 + dx, 4) * 4 + lax.rem(lax.rem(cx, 4) + dz, 4)
-
-    def peer_y(off):
-        dz, rest = off // 8, off % 8
-        dy, dc = rest // 2, rest % 2
-        zl, yy, cc = cy // 8, lax.rem(cy // 2, 4), lax.rem(cy, 2)
-        return lax.rem(zl + dz, 2) * 8 + lax.rem(yy + dy, 4) * 2 + lax.rem(cc + dc, 2)
-
-    def ring(n):
-        return min(n, 4 - n)
-
-    order_x = sorted(range(1, 16), key=lambda o: -(ring(o // 4) + 2 * ring(o % 4)))
-    order_y = sorted(range(1, 16), key=lambda o: -(3 * (o // 8) + 3 * ring((o % 8) // 2) + o % 2))
-
-    barrier = pltpu.get_barrier_semaphore()
-    for off in order_x:
-        pl.semaphore_signal(
-            barrier, inc=1, device_id=(peer_x(off), cy), device_id_type=pl.DeviceIdType.MESH
-        )
-    for off in order_y:
-        pl.semaphore_signal(
-            barrier, inc=1, device_id=(cx, peer_y(off)), device_id_type=pl.DeviceIdType.MESH
-        )
-
     def exchange(step, axis, src, dst):
         copies = []
         for off in order_x if axis == "gx" else order_y:
             if axis == "gx":
-                peer, me, device = peer_x(off), cx, (peer_x(off), cy)
+                peer, me, device = peer_x[off], cx, (peer_x[off], cy)
             else:
-                peer, me, device = peer_y(off), cy, (cx, peer_y(off))
+                peer, me, device = peer_y[off], cy, (cx, peer_y[off])
             copy = pltpu.make_async_remote_copy(
                 src_ref=src.at[peer],
                 dst_ref=dst.at[me],
@@ -283,8 +282,6 @@
         rows = slice(xy * WP, xy * WP + WP)
         local[xy] = jnp.dot(pw_back, sig[rows], preferred_element_type=F32)[0:W]
     from_cells(cells, outv)
-    put_out = pltpu.make_async_copy(outv, out_h, store_sem.at[0])
-    put_out.start()
     drain(c1)
     drain(c2)
     drain(c3)
@@ -324,9 +321,6 @@
         for s in range(2):
             for jt in range(4):
                 gs[jt, s, w] = parts[s][:, jt * WP : jt * WP + W]
-
-    put_gs = pltpu.make_async_copy(gs, gspec_h, store_sem.at[1])
-    put_gs.start()
 
     arrive(c6)
     x_inverse(z.at[1].reshape(128, 128), s4.reshape(256, 128))
@@ -341,27 +335,31 @@
             xy = half * 4 + sub
             cells[:, xy, :] = local[xy] + spatial[sub * WP : sub * WP + W]
     from_cells(cells, gout)
-    put_grad = pltpu.make_async_copy(gout, gfield_h, store_sem.at[2])
-    put_grad.start()
     drain(c7)
-    put_out.wait()
-    put_gs.wait()
-    put_grad.wait()
+
+
+def store_kernel(a, b, c, a_out, b_out, c_out, sems):
+    copies = [
+        pltpu.make_async_copy(src, dst, sems.at[i])
+        for i, (src, dst) in enumerate(((a, a_out), (b, b_out), (c, c_out)))
+    ]
+    for copy in copies:
+        copy.start()
+    for copy in copies:
+        copy.wait()
 
 
 def on_device(field, cotangent, spectral_weight, pointwise_weight, channel_bias):
     constants = tables()
     weight = jnp.transpose(spectral_weight, (0, 1, 2, 4, 5, 3)).reshape(4, 2, W, 16, W)
     hbm = pl.BlockSpec(memory_space=pltpu.MemorySpace.HBM)
-    out, gfield, gspec = pl.pallas_call(
+    vmem = pl.BlockSpec(memory_space=pltpu.MemorySpace.VMEM)
+    shapes = (((W, 2, 4, Q), BF16), ((W, 2, 4, Q), BF16), ((4, 2, W, 16, W), F32))
+    results = pl.pallas_call(
         kernel,
-        out_shape=(
-            jax.ShapeDtypeStruct((W, 2, 4, Q), BF16),
-            jax.ShapeDtypeStruct((W, 2, 4, Q), BF16),
-            jax.ShapeDtypeStruct((4, 2, W, 16, W), F32),
-        ),
+        out_shape=tuple(pltpu.VMEM(shape, dtype) for shape, dtype in shapes),
         in_specs=[hbm] * 10,
-        out_specs=(hbm,) * 3,
+        out_specs=(vmem,) * 3,
         scratch_shapes=[
             pltpu.VMEM((W, 2, 4, Q), BF16),
             pltpu.VMEM((W, 2, 4, Q), BF16),
@@ -381,9 +379,6 @@
             pltpu.VMEM((8, W, Q), F32),
             pltpu.VMEM((8, W, Q), F32),
             pltpu.VMEM((256, Q), BF16),
-            pltpu.VMEM((W, 2, 4, Q), BF16),
-            pltpu.VMEM((W, 2, 4, Q), BF16),
-            pltpu.VMEM((4, 2, W, 16, W), F32),
             pltpu.VMEM((32, 128), F32),
             pltpu.VMEM((16, 16, 128), F32),
             pltpu.VMEM((16, 8, 128), F32),
@@ -394,14 +389,21 @@
             pltpu.VMEM((2, 16, 8, 128), F32),
             pltpu.VMEM((2, 16, 16, 128), F32),
             pltpu.SemaphoreType.DMA((10,)),
-            pltpu.SemaphoreType.DMA((3,)),
             pltpu.SemaphoreType.DMA((8, 16)),
             pltpu.SemaphoreType.DMA((8, 16)),
         ],
         compiler_params=pltpu.CompilerParams(
-            collective_id=0, has_side_effects=True, vmem_limit_bytes=67043328
+            collective_id=0, has_side_effects=True, vmem_limit_bytes=VMEM - RESULTS
         ),
     )(field, cotangent, weight, pointwise_weight, channel_bias, *constants)
+    out, gfield, gspec = pl.pallas_call(
+        store_kernel,
+        out_shape=tuple(jax.ShapeDtypeStruct(shape, dtype) for shape, dtype in shapes),
+        in_specs=[pl.BlockSpec(memory_space=pl.ANY)] * 3,
+        out_specs=(hbm,) * 3,
+        scratch_shapes=[pltpu.SemaphoreType.DMA((3,))],
+        compiler_params=pltpu.CompilerParams(vmem_limit_bytes=1 << 20),
+    )(*results)
     grad = jnp.transpose(gspec.reshape(4, 2, W, 1, 16, W), (0, 1, 2, 5, 3, 4))
     return out, gfield, grad
 

time: 64.2 us -> 59 us (0.919)
  local copies, waits for them, and re-layouts: 5.73 us -> 0 us
  Pallas kernels: 57.6 us -> 58.3 us
    unnamed x3 -> x0, local copies, waits for them, and re-layouts: 5.73 us -> none
    pallas_call x1 -> x2, Pallas kernels: 57.6 us -> 58.3 us  [the longest x1 57.1 us: on_device(): pl.pallas_call(kernel, out_shape=tuple((pltpu.VMEM(shape, dtype) for shap...]
where the time goes in v5:
time: 59 us; the launch traced here: 58.9 us
  Pallas kernels  58.3 us (99%)
  between operations  0.64 us (1%)
    pallas_call x1, Pallas kernels, on_device(): pl.pallas_call(kernel, out_shape=tuple((pltpu.VMEM(shape, dtype) for shap...  57.1 us
    pallas_call x1, Pallas kernels, on_device(): pl.pallas_call(store_kernel, out_shape=tuple((jax.ShapeDtypeStruct(shape,...  1.19 us

profile of v5, /device:TPU:1, one launch (start us, length us, event | category | flops | bytes accessed | tf_op | source)
XLA Modules:
  0.0 58.9 jit_solution(10029571442752816782)
XLA Ops:
  0.6 57.1 %shard_map.121 = (bf16[20,2,4,512]{3,2,1,0:T(4,128)(2,1)S(1)}, bf16[20,2,4,512]{3,2,1,0:T(4,128)(2,1)S(1)}, f32[4,2,20,16,20]{4,3,2,1,0:T(8,128)S(1)}) custom-call(bf16[20,2,4,512]{3,2,1,0:T(4,128)(2,1)} %field.1, bf16[20,2,4,512]{3,2,1,0:T(4,128)(2,1)} %cot.1, f32[4,2,20,16,20]{4,3,2,1,0:T(8,128)} %bitcast.10, bf16[20,20]{1,0:T(8,128)(2,1)} %pw.1, f32[20]{0:T(128)} %bias.1, ...), custom_call_target="tpu_custom_call" | custom-call | tf_op jit(solution)/shard_map/pallas_call | solution.py:358
  57.7 1.2 %shard_map.122 = (bf16[20,2,4,512]{3,2,1,0:T(4,128)(2,1)}, bf16[20,2,4,512]{3,2,1,0:T(4,128)(2,1)}, f32[4,2,20,16,20]{4,3,2,1,0:T(8,128)}) custom-call(bf16[20,2,4,512]{3,2,1,0:T(4,128)(2,1)S(1)} %get-tuple-element.9.a, bf16[20,2,4,512]{3,2,1,0:T(4,128)(2,1)S(1)} %get-tuple-element.10.b, f32[4,2,20,16,20]{4,3,2,1,0:T(8,128)S(1)} %get-tuple-element.11.c), custom_call_target="tpu_custom_call" | custom-call | tf_op jit(solution)/shard_map/pallas_call | solution.py:399

commit v6 on v5

--- a/solution.py
+++ b/solution.py
@@ -87,8 +87,9 @@
     cy = lax.axis_index("gy")
 
     turn_x = [lax.rem(cx // 4 + i, 4) * 4 for i in range(4)]
-    turn_z = [lax.rem(lax.rem(cx, 4) + i, 4) for i in range(4)]
-    turn_l = [lax.rem(cy // 8 + i, 2) * 8 for i in range(2)]
+    low = cy // 8
+    turn_z = [lax.rem(lax.rem(cx, 4) + i + low * (4 - 2 * i), 4) for i in range(4)]
+    turn_l = [lax.rem(low + i, 2) * 8 for i in range(2)]
     turn_y = [lax.rem(cy // 2 + i, 4) * 2 for i in range(4)]
     turn_c = [lax.rem(cy + i, 2) for i in range(2)]
     peer_x = [turn_x[o // 4] + turn_z[o % 4] for o in range(16)]
@@ -97,15 +98,19 @@
     def ring(n):
         return min(n, 4 - n)
 
-    order_x = sorted(range(1, 16), key=lambda o: -(ring(o // 4) + 2 * ring(o % 4)))
+    order_x = sorted(range(16), key=lambda o: -(ring(o // 4) + (1, 3, 3, 1)[o % 4]))
     order_y = sorted(range(1, 16), key=lambda o: -(3 * (o // 8) + 3 * ring((o % 8) // 2) + o % 2))
 
+    other = turn_l[1] + lax.rem(cy, 8)
+    flip_y = [turn_l[1 - o // 8] + turn_y[(o % 8) // 2] + turn_c[o % 2] for o in range(16)]
     barrier = pltpu.get_barrier_semaphore()
     for off in order_x:
         pl.semaphore_signal(
-            barrier, inc=1, device_id=(peer_x[off], cy), device_id_type=pl.DeviceIdType.MESH
+            barrier, inc=1, device_id=(peer_x[off], other), device_id_type=pl.DeviceIdType.MESH
         )
     for off in order_y:
+        if off == 8:
+            continue
         pl.semaphore_signal(
             barrier, inc=1, device_id=(cx, peer_y[off]), device_id_type=pl.DeviceIdType.MESH
         )
@@ -118,25 +123,38 @@
     for copy in loads:
         copy.start()
 
-    def exchange(step, axis, src, dst):
-        copies = []
-        for off in order_x if axis == "gx" else order_y:
-            if axis == "gx":
-                peer, me, device = peer_x[off], cx, (peer_x[off], cy)
-            else:
-                peer, me, device = peer_y[off], cy, (cx, peer_y[off])
-            copy = pltpu.make_async_remote_copy(
-                src_ref=src.at[peer],
-                dst_ref=dst.at[me],
-                send_sem=send_sem.at[step, off],
-                recv_sem=recv_sem.at[step, off],
-                device_id=device,
-                device_id_type=pl.DeviceIdType.MESH,
+    def start(step, off, src, dst, device):
+        copy = pltpu.make_async_remote_copy(
+            src_ref=src,
+            dst_ref=dst,
+            send_sem=send_sem.at[step, off],
+            recv_sem=recv_sem.at[step, off],
+            device_id=device,
+            device_id_type=pl.DeviceIdType.MESH,
+        )
+        copy.start()
+        return copy
+
+    def exchange_x(step, src, dst):
+        return [
+            start(step, o, src.at[peer_x[o]], dst.at[cx], (peer_x[o], other)) for o in order_x
+        ]
+
+    def exchange_y(step, src, dst, inverse):
+        copies = [
+            start(
+                step,
+                o,
+                src.at[flip_y[o] if inverse else peer_y[o]],
+                dst.at[cy if inverse else other],
+                (cx, peer_y[o]),
             )
-            copy.start()
-            copies.append(copy)
-        me = cx if axis == "gx" else cy
-        dst[me] = src[me]
+            for o in order_y
+        ]
+        if inverse:
+            dst[cy] = src[other]
+        else:
+            dst[other] = src[cy]
         return copies
 
     def arrive(copies):
@@ -147,17 +165,17 @@
         for copy in copies:
             copy.wait_send()
 
-    def pack_modes(values, send):
+    def pack_modes(values, send, half):
         spectra = lax.dot_general(
-            zt[...], values[...], (((1,), (1,)), ((), ())), preferred_element_type=F32
+            zt[...],
+            values[half * 128 : half * 128 + 128],
+            (((1,), (1,)), ((), ())),
+            preferred_element_type=F32,
         )
-        for half in range(2):
-            parts = [
-                spectra[jt * 32 : jt * 32 + 32, half * 128 : half * 128 + 128] for jt in range(4)
-            ]
-            for sub, block in enumerate(block_transpose(parts)):
-                for s in range(2):
-                    send[:, s * 8 + half * 4 + sub, :] = block[s * 16 : s * 16 + 16]
+        parts = [spectra[jt * 32 : jt * 32 + 32] for jt in range(4)]
+        for sub, block in enumerate(block_transpose(parts)):
+            for s in range(2):
+                send[:, s * 8 + half * 4 + sub, :] = block[s * 16 : s * 16 + 16]
 
     def unpack_modes(recv, half):
         parts = [
@@ -207,9 +225,10 @@
     for xy in range(8):
         u[xy * WP : xy * WP + WP] = jnp.concatenate([cells[:, xy, :], pad], axis=0).astype(BF16)
     loads[1].wait()
-    pack_modes(u, s1)
+    for half in range(2):
+        pack_modes(u, s1, half)
     pl.semaphore_wait(barrier, 30)
-    c0 = exchange(0, "gx", s1, e.at[0])
+    c0 = exchange_x(0, s1, e.at[0])
 
     for copy in loads[2:]:
         copy.wait()
@@ -237,7 +256,7 @@
 
     arrive(c0)
     x_forward(e.at[0].reshape(256, 128), s2.reshape(128, 128))
-    c1 = exchange(1, "gy", s2, d.at[0])
+    c1 = exchange_y(1, s2, d.at[0], False)
     arrive(c1)
     spec[...] = matmul(ty, d[0].reshape(128, 128))
 
@@ -250,10 +269,10 @@
     mixed = jnp.concatenate([acc_r * kappa, acc_i * kappa], axis=0)
 
     s3[...] = matmul(tyi, mixed).reshape(16, 8, 128)
-    c2 = exchange(2, "gy", s3, z.at[0])
+    c2 = exchange_y(2, s3, z.at[0], True)
     arrive(c2)
     x_inverse(z.at[0].reshape(128, 128), s4.reshape(256, 128))
-    c3 = exchange(3, "gx", s4, v.at[0])
+    c3 = exchange_x(3, s4, v.at[0])
     drain(c0)
     arrive(c3)
 
@@ -271,9 +290,9 @@
             slope = t * (0.5 - b * t) + (b + 0.5)
             signal = ccells[:, xy, :] * slope
             sig[xy * WP : xy * WP + WP] = jnp.concatenate([signal, pad], axis=0).astype(BF16)
-
-    pack_modes(sig, s1)
-    c4 = exchange(4, "gx", s1, e.at[1])
+        pack_modes(sig, s1, half)
+
+    c4 = exchange_x(4, s1, e.at[1])
 
     for xy in range(8):
         p = pre[xy]
@@ -287,7 +306,7 @@
     drain(c3)
     arrive(c4)
     x_forward(e.at[1].reshape(256, 128), s2.reshape(128, 128))
-    c5 = exchange(5, "gy", s2, d.at[1])
+    c5 = exchange_y(5, s2, d.at[1], False)
     arrive(c5)
     back = matmul(ty, d[1].reshape(128, 128))
     br, bi = back[0:16] * kappa, back[16:32] * kappa
@@ -312,7 +331,7 @@
         return combine(a, b, h) if a is not None else None
 
     s3[...] = matmul(tyi, reduce_tree(0, 1)).reshape(16, 8, 128)
-    c6 = exchange(6, "gy", s3, z.at[1])
+    c6 = exchange_y(6, s3, z.at[1], True)
 
     @pl.loop(0, W)
     def _(w):
@@ -324,7 +343,7 @@
 
     arrive(c6)
     x_inverse(z.at[1].reshape(128, 128), s4.reshape(256, 128))
-    c7 = exchange(7, "gx", s4, v.at[1])
+    c7 = exchange_x(7, s4, v.at[1])
     drain(c4)
     drain(c5)
     drain(c6)

time: 59 us -> 57.3 us (0.971)
  Pallas kernels: 58.3 us -> 56.5 us
    pallas_call x1, Pallas kernels: 57.1 us -> 55.3 us  [on_device(): pl.pallas_call(kernel, out_shape=tuple((pltpu.VMEM(shape, dtype) for shap...]
where the time goes in v6:
time: 57.3 us; the launch traced here: 57.2 us
  Pallas kernels  56.5 us (99%)
  between operations  0.64 us (1%)
    pallas_call x1, Pallas kernels, on_device(): pl.pallas_call(kernel, out_shape=tuple((pltpu.VMEM(shape, dtype) for shap...  55.3 us
    pallas_call x1, Pallas kernels, on_device(): pl.pallas_call(store_kernel, out_shape=tuple((jax.ShapeDtypeStruct(shape,...  1.19 us

profile of v6, /device:TPU:1, one launch (start us, length us, event | category | flops | bytes accessed | tf_op | source)
XLA Modules:
  0.0 57.2 jit_solution(9035258476539144504)
XLA Ops:
  0.6 55.3 %shard_map.121 = (bf16[20,2,4,512]{3,2,1,0:T(4,128)(2,1)S(1)}, bf16[20,2,4,512]{3,2,1,0:T(4,128)(2,1)S(1)}, f32[4,2,20,16,20]{4,3,2,1,0:T(8,128)S(1)}) custom-call(bf16[20,2,4,512]{3,2,1,0:T(4,128)(2,1)} %field.1, bf16[20,2,4,512]{3,2,1,0:T(4,128)(2,1)} %cot.1, f32[4,2,20,16,20]{4,3,2,1,0:T(8,128)} %bitcast.10, bf16[20,20]{1,0:T(8,128)(2,1)} %pw.1, f32[20]{0:T(128)} %bias.1, ...), custom_call_target="tpu_custom_call" | custom-call | tf_op jit(solution)/shard_map/pallas_call | solution.py:377
  56.0 1.2 %shard_map.122 = (bf16[20,2,4,512]{3,2,1,0:T(4,128)(2,1)}, bf16[20,2,4,512]{3,2,1,0:T(4,128)(2,1)}, f32[4,2,20,16,20]{4,3,2,1,0:T(8,128)}) custom-call(bf16[20,2,4,512]{3,2,1,0:T(4,128)(2,1)S(1)} %get-tuple-element.9.a, bf16[20,2,4,512]{3,2,1,0:T(4,128)(2,1)S(1)} %get-tuple-element.10.b, f32[4,2,20,16,20]{4,3,2,1,0:T(8,128)S(1)} %get-tuple-element.11.c), custom_call_target="tpu_custom_call" | custom-call | tf_op jit(solution)/shard_map/pallas_call | solution.py:418

commit v7 on v6

--- a/solution.py
+++ b/solution.py
@@ -101,15 +101,15 @@
     order_x = sorted(range(16), key=lambda o: -(ring(o // 4) + (1, 3, 3, 1)[o % 4]))
     order_y = sorted(range(1, 16), key=lambda o: -(3 * (o // 8) + 3 * ring((o % 8) // 2) + o % 2))
 
-    other = turn_l[1] + lax.rem(cy, 8)
-    flip_y = [turn_l[1 - o // 8] + turn_y[(o % 8) // 2] + turn_c[o % 2] for o in range(16)]
+    other = turn_l[1] + turn_y[0] + turn_c[1]
+    flip_y = [turn_l[1 - o // 8] + turn_y[(o % 8) // 2] + turn_c[1 - o % 2] for o in range(16)]
     barrier = pltpu.get_barrier_semaphore()
     for off in order_x:
         pl.semaphore_signal(
             barrier, inc=1, device_id=(peer_x[off], other), device_id_type=pl.DeviceIdType.MESH
         )
     for off in order_y:
-        if off == 8:
+        if off == 9:
             continue
         pl.semaphore_signal(
             barrier, inc=1, device_id=(cx, peer_y[off]), device_id_type=pl.DeviceIdType.MESH

time: 57.3 us -> 59 us (1.030)
  Pallas kernels: 56.5 us -> 58.3 us
    pallas_call x1, Pallas kernels: 55.3 us -> 57.1 us  [on_device(): pl.pallas_call(kernel, out_shape=tuple((pltpu.VMEM(shape, dtype) for shap...]
where the time goes in v7:
time: 59 us; the launch traced here: 58.9 us
  Pallas kernels  58.3 us (99%)
  between operations  0.64 us (1%)
    pallas_call x1, Pallas kernels, on_device(): pl.pallas_call(kernel, out_shape=tuple((pltpu.VMEM(shape, dtype) for shap...  57.1 us
    pallas_call x1, Pallas kernels, on_device(): pl.pallas_call(store_kernel, out_shape=tuple((jax.ShapeDtypeStruct(shape,...  1.19 us

profile of v7, /device:TPU:1, one launch (start us, length us, event | category | flops | bytes accessed | tf_op | source)
XLA Modules:
  0.0 58.9 jit_solution(14560967706862098380)
XLA Ops:
  0.6 57.1 %shard_map.121 = (bf16[20,2,4,512]{3,2,1,0:T(4,128)(2,1)S(1)}, bf16[20,2,4,512]{3,2,1,0:T(4,128)(2,1)S(1)}, f32[4,2,20,16,20]{4,3,2,1,0:T(8,128)S(1)}) custom-call(bf16[20,2,4,512]{3,2,1,0:T(4,128)(2,1)} %field.1, bf16[20,2,4,512]{3,2,1,0:T(4,128)(2,1)} %cot.1, f32[4,2,20,16,20]{4,3,2,1,0:T(8,128)} %bitcast.10, bf16[20,20]{1,0:T(8,128)(2,1)} %pw.1, f32[20]{0:T(128)} %bias.1, ...), custom_call_target="tpu_custom_call" | custom-call | tf_op jit(solution)/shard_map/pallas_call | solution.py:377
  57.7 1.2 %shard_map.122 = (bf16[20,2,4,512]{3,2,1,0:T(4,128)(2,1)}, bf16[20,2,4,512]{3,2,1,0:T(4,128)(2,1)}, f32[4,2,20,16,20]{4,3,2,1,0:T(8,128)}) custom-call(bf16[20,2,4,512]{3,2,1,0:T(4,128)(2,1)S(1)} %get-tuple-element.9.a, bf16[20,2,4,512]{3,2,1,0:T(4,128)(2,1)S(1)} %get-tuple-element.10.b, f32[4,2,20,16,20]{4,3,2,1,0:T(8,128)S(1)} %get-tuple-element.11.c), custom_call_target="tpu_custom_call" | custom-call | tf_op jit(solution)/shard_map/pallas_call | solution.py:418

commit v8 on v6

--- a/solution.py
+++ b/solution.py
@@ -40,13 +40,13 @@
 
 def tables():
     fx = rotation_blocks(32, -1.0).reshape(2, 2, 16, 16, 2)
-    tx = np.einsum("rskcx->krcsx", fx).reshape(32, 64)
+    tx = np.einsum("rskcx->krsxc", fx).reshape(32, 64)
     fy = rotation_blocks(64, -1.0).reshape(2, 2, 16, 16, 4)
     ty = np.einsum("rskpy->rkpsy", fy).reshape(32, 128)
     iy = rotation_blocks(64, 1.0).reshape(2, 2, 16, 16, 4)
     tyi = np.einsum("rskpy->prysk", iy).reshape(128, 32)
     ix = rotation_blocks(32, 1.0).reshape(2, 2, 16, 16, 2)
-    txi = np.einsum("rskcx->crxks", ix).reshape(64, 32)
+    txi = np.einsum("rskcx->rxcks", ix).reshape(64, 32)
     z, t = np.arange(32), np.arange(16)
     f = frequencies()
     phase = (
@@ -165,7 +165,42 @@
         for copy in copies:
             copy.wait_send()
 
-    def pack_modes(values, send, half):
+    in_block = lax.rem(lax.broadcasted_iota(jnp.int32, (16, 128), 1), WP)
+    lane_from = {n: in_block >= n for n in (4, 8, 12, 16, 24, 28) + (W,)}
+
+    def store_cells(blocks, send):
+        for s in range(2):
+            c = blocks[s]
+
+            def moved(cell, shift):
+                return pltpu.roll(c[cell], shift, 1)
+
+            fill = (
+                moved(5, 20),
+                jnp.where(lane_from[28], moved(6, 28), moved(5, 8)),
+                moved(6, 16),
+                jnp.where(lane_from[24], moved(7, 24), moved(6, 4)),
+                moved(7, 12),
+            )
+            for i in range(5):
+                send[:, s * 5 + i, :] = jnp.where(lane_from[W], fill[i], c[i])
+
+    def load_cells(recv):
+        blocks = []
+        for s in range(2):
+            c = [recv[:, s * 5 + i, :] for i in range(5)]
+
+            def moved(row, shift):
+                return pltpu.roll(c[row], 128 - shift, 1)
+
+            five = jnp.where(lane_from[12], moved(1, 8), moved(0, 20))
+            six = jnp.where(lane_from[4], moved(2, 16), moved(1, 28))
+            six = jnp.where(lane_from[16], moved(3, 4), six)
+            seven = jnp.where(lane_from[8], moved(4, 12), moved(3, 24))
+            blocks.append(c + [five, six, seven])
+        return blocks
+
+    def pack_modes(values, half):
         spectra = lax.dot_general(
             zt[...],
             values[half * 128 : half * 128 + 128],
@@ -173,13 +208,12 @@
             preferred_element_type=F32,
         )
         parts = [spectra[jt * 32 : jt * 32 + 32] for jt in range(4)]
-        for sub, block in enumerate(block_transpose(parts)):
-            for s in range(2):
-                send[:, s * 8 + half * 4 + sub, :] = block[s * 16 : s * 16 + 16]
-
-    def unpack_modes(recv, half):
+        turned = block_transpose(parts)
+        return [[block[s * 16 : s * 16 + 16] for block in turned] for s in range(2)]
+
+    def unpack_modes(blocks, half):
         parts = [
-            jnp.concatenate([recv[:, s * 8 + half * 4 + sub, :] for s in range(2)], axis=0)
+            jnp.concatenate([blocks[s][half * 4 + sub] for s in range(2)], axis=0)
             for sub in range(4)
         ]
         stacked = jnp.concatenate(block_transpose(parts), axis=0)
@@ -192,18 +226,30 @@
             table[...], jnp.concatenate([hi, hi, lo], axis=0), preferred_element_type=F32
         )
 
-    def y_to_lanes(recv, n):
-        return jnp.concatenate([recv[pl.ds(y, n, stride=4), :] for y in range(4)], axis=1)
-
     def x_forward(recv, send):
-        out = matmul(tx, y_to_lanes(recv, 64))
+        blocks = load_cells(recv)
+        columns = [
+            jnp.concatenate([blocks[s][x * 4 + y] for s in range(2) for x in range(2)], axis=0)
+            for y in range(4)
+        ]
+        out = matmul(tx, jnp.concatenate(columns, axis=1))
         for y in range(4):
             send[pl.ds(y, 32, stride=4), :] = out[:, y * 128 : y * 128 + 128]
 
     def x_inverse(recv, send):
-        out = matmul(txi, y_to_lanes(recv, 32))
-        for y in range(4):
-            send[pl.ds(y, 64, stride=4), :] = out[:, y * 128 : y * 128 + 128]
+        columns = [recv[pl.ds(y, 32, stride=4), :] for y in range(4)]
+        out = matmul(txi, jnp.concatenate(columns, axis=1))
+        store_cells(
+            [
+                [
+                    out[(r * 2 + x) * 16 : (r * 2 + x) * 16 + 16, y * 128 : y * 128 + 128]
+                    for x in range(2)
+                    for y in range(4)
+                ]
+                for r in range(2)
+            ],
+            send,
+        )
 
     def to_cells(source, target):
         for x in range(2):
@@ -225,8 +271,8 @@
     for xy in range(8):
         u[xy * WP : xy * WP + WP] = jnp.concatenate([cells[:, xy, :], pad], axis=0).astype(BF16)
     loads[1].wait()
-    for half in range(2):
-        pack_modes(u, s1, half)
+    first, second = pack_modes(u, 0), pack_modes(u, 1)
+    store_cells([first[s] + second[s] for s in range(2)], s1)
     pl.semaphore_wait(barrier, 30)
     c0 = exchange_x(0, s1, e.at[0])
 
@@ -255,7 +301,7 @@
     to_cells(cin, ccells)
 
     arrive(c0)
-    x_forward(e.at[0].reshape(256, 128), s2.reshape(128, 128))
+    x_forward(e.at[0], s2.reshape(128, 128))
     c1 = exchange_y(1, s2, d.at[0], False)
     arrive(c1)
     spec[...] = matmul(ty, d[0].reshape(128, 128))
@@ -271,15 +317,17 @@
     s3[...] = matmul(tyi, mixed).reshape(16, 8, 128)
     c2 = exchange_y(2, s3, z.at[0], True)
     arrive(c2)
-    x_inverse(z.at[0].reshape(128, 128), s4.reshape(256, 128))
+    x_inverse(z.at[0].reshape(128, 128), s4)
     c3 = exchange_x(3, s4, v.at[0])
     drain(c0)
     arrive(c3)
 
     root = math.sqrt(2.0 / math.pi)
     cubic = 0.044715
+    arrived = load_cells(v.at[0])
+    packed = []
     for half in range(2):
-        spatial = jnp.dot(unpack_modes(v.at[0], half), zt[...], preferred_element_type=F32)
+        spatial = jnp.dot(unpack_modes(arrived, half), zt[...], preferred_element_type=F32)
         for sub in range(4):
             xy = half * 4 + sub
             p = local[xy] + spatial[sub * WP : sub * WP + W]
@@ -290,8 +338,9 @@
             slope = t * (0.5 - b * t) + (b + 0.5)
             signal = ccells[:, xy, :] * slope
             sig[xy * WP : xy * WP + WP] = jnp.concatenate([signal, pad], axis=0).astype(BF16)
-        pack_modes(sig, s1, half)
-
+        packed.append(pack_modes(sig, half))
+
+    store_cells([packed[0][s] + packed[1][s] for s in range(2)], s1)
     c4 = exchange_x(4, s1, e.at[1])
 
     for xy in range(8):
@@ -305,7 +354,7 @@
     drain(c2)
     drain(c3)
     arrive(c4)
-    x_forward(e.at[1].reshape(256, 128), s2.reshape(128, 128))
+    x_forward(e.at[1], s2.reshape(128, 128))
     c5 = exchange_y(5, s2, d.at[1], False)
     arrive(c5)
     back = matmul(ty, d[1].reshape(128, 128))
@@ -342,14 +391,15 @@
                 gs[jt, s, w] = parts[s][:, jt * WP : jt * WP + W]
 
     arrive(c6)
-    x_inverse(z.at[1].reshape(128, 128), s4.reshape(256, 128))
+    x_inverse(z.at[1].reshape(128, 128), s4)
     c7 = exchange_x(7, s4, v.at[1])
     drain(c4)
     drain(c5)
     drain(c6)
     arrive(c7)
+    arrived = load_cells(v.at[1])
     for half in range(2):
-        spatial = jnp.dot(unpack_modes(v.at[1], half), zt[...], preferred_element_type=F32)
+        spatial = jnp.dot(unpack_modes(arrived, half), zt[...], preferred_element_type=F32)
         for sub in range(4):
             xy = half * 4 + sub
             cells[:, xy, :] = local[xy] + spatial[sub * WP : sub * WP + W]
@@ -399,14 +449,14 @@
             pltpu.VMEM((8, W, Q), F32),
             pltpu.VMEM((256, Q), BF16),
             pltpu.VMEM((32, 128), F32),
-            pltpu.VMEM((16, 16, 128), F32),
+            pltpu.VMEM((16, 10, 128), F32),
             pltpu.VMEM((16, 8, 128), F32),
             pltpu.VMEM((16, 8, 128), F32),
-            pltpu.VMEM((16, 16, 128), F32),
-            pltpu.VMEM((2, 16, 16, 128), F32),
+            pltpu.VMEM((16, 10, 128), F32),
+            pltpu.VMEM((2, 16, 10, 128), F32),
             pltpu.VMEM((2, 16, 8, 128), F32),
             pltpu.VMEM((2, 16, 8, 128), F32),
-            pltpu.VMEM((2, 16, 16, 128), F32),
+            pltpu.VMEM((2, 16, 10, 128), F32),
             pltpu.SemaphoreType.DMA((10,)),
             pltpu.SemaphoreType.DMA((8, 16)),
             pltpu.SemaphoreType.DMA((8, 16)),

time: 57.3 us -> 56 us (0.977)
  Pallas kernels: 56.5 us -> 55.3 us
    pallas_call x1, Pallas kernels: 55.3 us -> 54.1 us  [on_device(): pl.pallas_call(kernel, out_shape=tuple((pltpu.VMEM(shape, dtype) for shap...]
where the time goes in v8:
time: 56 us; the launch traced here: 55.9 us
  Pallas kernels  55.3 us (99%)
  between operations  0.64 us (1%)
    pallas_call x1, Pallas kernels, on_device(): pl.pallas_call(kernel, out_shape=tuple((pltpu.VMEM(shape, dtype) for shap...  54.1 us
    pallas_call x1, Pallas kernels, on_device(): pl.pallas_call(store_kernel, out_shape=tuple((jax.ShapeDtypeStruct(shape,...  1.19 us

profile of v8, /device:TPU:1, one launch (start us, length us, event | category | flops | bytes accessed | tf_op | source)
XLA Modules:
  0.0 55.9 jit_solution(5432396592753241657)
XLA Ops:
  0.6 54.1 %shard_map.121 = (bf16[20,2,4,512]{3,2,1,0:T(4,128)(2,1)S(1)}, bf16[20,2,4,512]{3,2,1,0:T(4,128)(2,1)S(1)}, f32[4,2,20,16,20]{4,3,2,1,0:T(8,128)S(1)}) custom-call(bf16[20,2,4,512]{3,2,1,0:T(4,128)(2,1)} %field.1, bf16[20,2,4,512]{3,2,1,0:T(4,128)(2,1)} %cot.1, f32[4,2,20,16,20]{4,3,2,1,0:T(8,128)} %bitcast.10, bf16[20,20]{1,0:T(8,128)(2,1)} %pw.1, f32[20]{0:T(128)} %bias.1, ...), custom_call_target="tpu_custom_call" | custom-call | tf_op jit(solution)/shard_map/pallas_call | solution.py:427
  54.7 1.2 %shard_map.122 = (bf16[20,2,4,512]{3,2,1,0:T(4,128)(2,1)}, bf16[20,2,4,512]{3,2,1,0:T(4,128)(2,1)}, f32[4,2,20,16,20]{4,3,2,1,0:T(8,128)}) custom-call(bf16[20,2,4,512]{3,2,1,0:T(4,128)(2,1)S(1)} %get-tuple-element.9.a, bf16[20,2,4,512]{3,2,1,0:T(4,128)(2,1)S(1)} %get-tuple-element.10.b, f32[4,2,20,16,20]{4,3,2,1,0:T(8,128)S(1)} %get-tuple-element.11.c), custom_call_target="tpu_custom_call" | custom-call | tf_op jit(solution)/shard_map/pallas_call | solution.py:468

commit v9 on v8

--- a/solution.py
+++ b/solution.py
@@ -135,9 +135,12 @@
         copy.start()
         return copy
 
+    used = pl.ds(0, 10)
+
     def exchange_x(step, src, dst):
         return [
-            start(step, o, src.at[peer_x[o]], dst.at[cx], (peer_x[o], other)) for o in order_x
+            start(step, o, src.at[peer_x[o], used], dst.at[cx, used], (peer_x[o], other))
+            for o in order_x
         ]
 
     def exchange_y(step, src, dst, inverse):
@@ -169,6 +172,7 @@
     lane_from = {n: in_block >= n for n in (4, 8, 12, 16, 24, 28) + (W,)}
 
     def store_cells(blocks, send):
+        rows = send.reshape(256, 128)
         for s in range(2):
             c = blocks[s]
 
@@ -183,12 +187,13 @@
                 moved(7, 12),
             )
             for i in range(5):
-                send[:, s * 5 + i, :] = jnp.where(lane_from[W], fill[i], c[i])
+                rows[pl.ds(s * 5 + i, 16, stride=16), :] = jnp.where(lane_from[W], fill[i], c[i])
 
     def load_cells(recv):
         blocks = []
+        rows = recv.reshape(256, 128)
         for s in range(2):
-            c = [recv[:, s * 5 + i, :] for i in range(5)]
+            c = [rows[pl.ds(s * 5 + i, 16, stride=16), :] for i in range(5)]
 
             def moved(row, shift):
                 return pltpu.roll(c[row], 128 - shift, 1)
@@ -251,13 +256,28 @@
             send,
         )
 
+    def lanes(i):
+        return slice(i * 128, i * 128 + 128)
+
     def to_cells(source, target):
         for x in range(2):
-            target[:, 4 * x : 4 * x + 4, :] = source[:, x].astype(F32)
+            value = source[:, x].astype(F32)
+            for i in range(4):
+                target.at[i].reshape(W, 8, 128)[:, 4 * x : 4 * x + 4, :] = value[:, :, lanes(i)]
 
     def from_cells(source, target):
         for x in range(2):
-            target[:, x] = source[:, 4 * x : 4 * x + 4, :].astype(BF16)
+            parts = [
+                source.at[i].reshape(W, 8, 128)[:, 4 * x : 4 * x + 4, :] for i in range(4)
+            ]
+            target[:, x] = jnp.concatenate(parts, axis=2).astype(BF16)
+
+    def load_cell(rows, xy):
+        return jnp.concatenate([rows[i, pl.ds(xy, W, stride=8), :] for i in range(4)], axis=1)
+
+    def store_cell(rows, xy, value):
+        for i in range(4):
+            rows[i, pl.ds(xy, W, stride=8), :] = value[:, lanes(i)]
 
     kappa = jnp.where(lax.broadcasted_iota(jnp.int32, (16, 128), 1) < WP, 1.0, 2.0).astype(F32)
     gather_base = lane_blocks(16) * WP
@@ -269,7 +289,7 @@
     to_cells(fin, cells)
     pad = jnp.zeros((WP - W, Q), F32)
     for xy in range(8):
-        u[xy * WP : xy * WP + WP] = jnp.concatenate([cells[:, xy, :], pad], axis=0).astype(BF16)
+        u[xy * WP : xy * WP + WP] = jnp.concatenate([load_cell(cells, xy), pad], axis=0).astype(BF16)
     loads[1].wait()
     first, second = pack_modes(u, 0), pack_modes(u, 1)
     store_cells([first[s] + second[s] for s in range(2)], s1)
@@ -336,7 +356,7 @@
             t = jnp.tanh(p * (root * cubic * p2 + root))
             b = p * (1.5 * root * cubic * p2 + 0.5 * root)
             slope = t * (0.5 - b * t) + (b + 0.5)
-            signal = ccells[:, xy, :] * slope
+            signal = load_cell(ccells, xy) * slope
             sig[xy * WP : xy * WP + WP] = jnp.concatenate([signal, pad], axis=0).astype(BF16)
         packed.append(pack_modes(sig, half))
 
@@ -346,7 +366,7 @@
     for xy in range(8):
         p = pre[xy]
         t = jnp.tanh(p * (root * cubic * (p * p) + root))
-        cells[:, xy, :] = 0.5 * p * (1.0 + t)
+        store_cell(cells, xy, 0.5 * p * (1.0 + t))
         rows = slice(xy * WP, xy * WP + WP)
         local[xy] = jnp.dot(pw_back, sig[rows], preferred_element_type=F32)[0:W]
     from_cells(cells, outv)
@@ -402,7 +422,7 @@
         spatial = jnp.dot(unpack_modes(arrived, half), zt[...], preferred_element_type=F32)
         for sub in range(4):
             xy = half * 4 + sub
-            cells[:, xy, :] = local[xy] + spatial[sub * WP : sub * WP + W]
+            store_cell(cells, xy, local[xy] + spatial[sub * WP : sub * WP + W])
     from_cells(cells, gout)
     drain(c7)
 
@@ -441,22 +461,22 @@
             pltpu.VMEM((128, 96), BF16),
             pltpu.VMEM((64, 96), BF16),
             pltpu.VMEM((256, Q), BF16),
-            pltpu.VMEM((W, 8, Q), F32),
-            pltpu.VMEM((W, 8, Q), F32),
+            pltpu.VMEM((4, W * 8, 128), F32),
+            pltpu.VMEM((4, W * 8, 128), F32),
             pltpu.VMEM((128, 128), F32),
             pltpu.VMEM((2, W, 16, 128), F32),
             pltpu.VMEM((8, W, Q), F32),
             pltpu.VMEM((8, W, Q), F32),
             pltpu.VMEM((256, Q), BF16),
             pltpu.VMEM((32, 128), F32),
-            pltpu.VMEM((16, 10, 128), F32),
+            pltpu.VMEM((16, 16, 128), F32),
             pltpu.VMEM((16, 8, 128), F32),
             pltpu.VMEM((16, 8, 128), F32),
-            pltpu.VMEM((16, 10, 128), F32),
-            pltpu.VMEM((2, 16, 10, 128), F32),
+            pltpu.VMEM((16, 16, 128), F32),
+            pltpu.VMEM((2, 16, 16, 128), F32),
             pltpu.VMEM((2, 16, 8, 128), F32),
             pltpu.VMEM((2, 16, 8, 128), F32),
-            pltpu.VMEM((2, 16, 10, 128), F32),
+            pltpu.VMEM((2, 16, 16, 128), F32),
             pltpu.SemaphoreType.DMA((10,)),
             pltpu.SemaphoreType.DMA((8, 16)),
             pltpu.SemaphoreType.DMA((8, 16)),

time: 56 us -> 55.9 us (level)
  no operation moved by 1% of the time
where the time goes in v9:
time: 55.9 us; the launch traced here: 55.8 us
  Pallas kernels  55.2 us (99%)
  between operations  0.64 us (1%)
    pallas_call x1, Pallas kernels, on_device(): pl.pallas_call(kernel, out_shape=tuple((pltpu.VMEM(shape, dtype) for shap...  54 us
    pallas_call x1, Pallas kernels, on_device(): pl.pallas_call(store_kernel, out_shape=tuple((jax.ShapeDtypeStruct(shape,...  1.19 us

profile of v9, /device:TPU:1, one launch (start us, length us, event | category | flops | bytes accessed | tf_op | source)
XLA Modules:
  0.0 55.8 jit_solution(372904812587792397)
XLA Ops:
  0.6 54.0 %shard_map.121 = (bf16[20,2,4,512]{3,2,1,0:T(4,128)(2,1)S(1)}, bf16[20,2,4,512]{3,2,1,0:T(4,128)(2,1)S(1)}, f32[4,2,20,16,20]{4,3,2,1,0:T(8,128)S(1)}) custom-call(bf16[20,2,4,512]{3,2,1,0:T(4,128)(2,1)} %field.1, bf16[20,2,4,512]{3,2,1,0:T(4,128)(2,1)} %cot.1, f32[4,2,20,16,20]{4,3,2,1,0:T(8,128)} %bitcast.10, bf16[20,20]{1,0:T(8,128)(2,1)} %pw.1, f32[20]{0:T(128)} %bias.1, ...), custom_call_target="tpu_custom_call" | custom-call | tf_op jit(solution)/shard_map/pallas_call | solution.py:447
  54.6 1.2 %shard_map.122 = (bf16[20,2,4,512]{3,2,1,0:T(4,128)(2,1)}, bf16[20,2,4,512]{3,2,1,0:T(4,128)(2,1)}, f32[4,2,20,16,20]{4,3,2,1,0:T(8,128)}) custom-call(bf16[20,2,4,512]{3,2,1,0:T(4,128)(2,1)S(1)} %get-tuple-element.9.a, bf16[20,2,4,512]{3,2,1,0:T(4,128)(2,1)S(1)} %get-tuple-element.10.b, f32[4,2,20,16,20]{4,3,2,1,0:T(8,128)S(1)} %get-tuple-element.11.c), custom_call_target="tpu_custom_call" | custom-call | tf_op jit(solution)/shard_map/pallas_call | solution.py:488

commit v10 on v9

--- a/solution.py
+++ b/solution.py
@@ -16,7 +16,7 @@
 F32 = jnp.float32
 BF16 = jnp.bfloat16
 VMEM = 67043328
-RESULTS = 2 * 20 * 8 * 512 * 2 + 160 * 16 * 128 * 4
+RESULTS = 20 * 8 * 512 * 2 + 160 * 16 * 128 * 4 + 256 * 512 + 192 * 512 * 4 + 128 * 512 * 2
 
 
 def frequencies():
@@ -75,11 +75,60 @@
     return out
 
 
+def lane_masks():
+    in_block = lax.rem(lax.broadcasted_iota(jnp.int32, (16, 128), 1), WP)
+    return {n: in_block >= n for n in (4, 8, 12, 16, 24, 28) + (W,)}
+
+
+def load_cells(recv):
+    from_lane = lane_masks()
+    blocks = []
+    rows = recv.reshape(256, 128)
+    for s in range(2):
+        c = [rows[pl.ds(s * 5 + i, 16, stride=16), :] for i in range(5)]
+
+        def moved(row, shift):
+            return pltpu.roll(c[row], 128 - shift, 1)
+
+        five = jnp.where(from_lane[12], moved(1, 8), moved(0, 20))
+        six = jnp.where(from_lane[4], moved(2, 16), moved(1, 28))
+        six = jnp.where(from_lane[16], moved(3, 4), six)
+        seven = jnp.where(from_lane[8], moved(4, 12), moved(3, 24))
+        blocks.append(c + [five, six, seven])
+    return blocks
+
+
+def unpack_modes(blocks, half):
+    parts = [
+        jnp.concatenate([blocks[s][half * 4 + sub] for s in range(2)], axis=0)
+        for sub in range(4)
+    ]
+    stacked = jnp.concatenate(block_transpose(parts), axis=0)
+    return stacked.T.astype(BF16)
+
+
+def lanes(i):
+    return slice(i * 128, i * 128 + 128)
+
+
+def from_cells(source, target):
+    for x in range(2):
+        parts = [
+            source.at[i].reshape(W, 8, 128)[:, 4 * x : 4 * x + 4, :] for i in range(4)
+        ]
+        target[:, x] = jnp.concatenate(parts, axis=2).astype(BF16)
+
+
+def store_cell(rows, xy, value):
+    for i in range(4):
+        rows[i, pl.ds(xy, W, stride=8), :] = value[:, lanes(i)]
+
+
 def kernel(
     field, cot, weight, pw, bias, zt_h, tx_h, ty_h, tyi_h, txi_h,
-    outv, gout, gs,
-    fin, cin, wv, pwv, bv, zt, tx, ty, tyi, txi,
-    u, cells, ccells, square, wt, local, pre, sig, spec,
+    outv, gs, vout, local, zt,
+    fin, cin, wv, pwv, bv, tx, ty, tyi, txi,
+    u, cells, ccells, square, wt, pre, sig, spec,
     s1, s2, s3, s4, e, d, z, v,
     load_sem, send_sem, recv_sem,
 ):
@@ -168,8 +217,7 @@
         for copy in copies:
             copy.wait_send()
 
-    in_block = lax.rem(lax.broadcasted_iota(jnp.int32, (16, 128), 1), WP)
-    lane_from = {n: in_block >= n for n in (4, 8, 12, 16, 24, 28) + (W,)}
+    lane_from = lane_masks()
 
     def store_cells(blocks, send):
         rows = send.reshape(256, 128)
@@ -188,22 +236,6 @@
             )
             for i in range(5):
                 rows[pl.ds(s * 5 + i, 16, stride=16), :] = jnp.where(lane_from[W], fill[i], c[i])
-
-    def load_cells(recv):
-        blocks = []
-        rows = recv.reshape(256, 128)
-        for s in range(2):
-            c = [rows[pl.ds(s * 5 + i, 16, stride=16), :] for i in range(5)]
-
-            def moved(row, shift):
-                return pltpu.roll(c[row], 128 - shift, 1)
-
-            five = jnp.where(lane_from[12], moved(1, 8), moved(0, 20))
-            six = jnp.where(lane_from[4], moved(2, 16), moved(1, 28))
-            six = jnp.where(lane_from[16], moved(3, 4), six)
-            seven = jnp.where(lane_from[8], moved(4, 12), moved(3, 24))
-            blocks.append(c + [five, six, seven])
-        return blocks
 
     def pack_modes(values, half):
         spectra = lax.dot_general(
@@ -215,14 +247,6 @@
         parts = [spectra[jt * 32 : jt * 32 + 32] for jt in range(4)]
         turned = block_transpose(parts)
         return [[block[s * 16 : s * 16 + 16] for block in turned] for s in range(2)]
-
-    def unpack_modes(blocks, half):
-        parts = [
-            jnp.concatenate([blocks[s][half * 4 + sub] for s in range(2)], axis=0)
-            for sub in range(4)
-        ]
-        stacked = jnp.concatenate(block_transpose(parts), axis=0)
-        return stacked.T.astype(BF16)
 
     def matmul(table, b):
         hi = b.astype(BF16)
@@ -256,28 +280,14 @@
             send,
         )
 
-    def lanes(i):
-        return slice(i * 128, i * 128 + 128)
-
     def to_cells(source, target):
         for x in range(2):
             value = source[:, x].astype(F32)
             for i in range(4):
                 target.at[i].reshape(W, 8, 128)[:, 4 * x : 4 * x + 4, :] = value[:, :, lanes(i)]
 
-    def from_cells(source, target):
-        for x in range(2):
-            parts = [
-                source.at[i].reshape(W, 8, 128)[:, 4 * x : 4 * x + 4, :] for i in range(4)
-            ]
-            target[:, x] = jnp.concatenate(parts, axis=2).astype(BF16)
-
     def load_cell(rows, xy):
         return jnp.concatenate([rows[i, pl.ds(xy, W, stride=8), :] for i in range(4)], axis=1)
-
-    def store_cell(rows, xy, value):
-        for i in range(4):
-            rows[i, pl.ds(xy, W, stride=8), :] = value[:, lanes(i)]
 
     kappa = jnp.where(lax.broadcasted_iota(jnp.int32, (16, 128), 1) < WP, 1.0, 2.0).astype(F32)
     gather_base = lane_blocks(16) * WP
@@ -346,8 +356,10 @@
     cubic = 0.044715
     arrived = load_cells(v.at[0])
     packed = []
+    both = jnp.concatenate([unpack_modes(arrived, half) for half in range(2)], axis=0)
+    both = jnp.dot(both, zt[...], preferred_element_type=F32)
     for half in range(2):
-        spatial = jnp.dot(unpack_modes(arrived, half), zt[...], preferred_element_type=F32)
+        spatial = both[half * 128 : half * 128 + 128]
         for sub in range(4):
             xy = half * 4 + sub
             p = local[xy] + spatial[sub * WP : sub * WP + W]
@@ -363,13 +375,16 @@
     store_cells([packed[0][s] + packed[1][s] for s in range(2)], s1)
     c4 = exchange_x(4, s1, e.at[1])
 
-    for xy in range(8):
-        p = pre[xy]
-        t = jnp.tanh(p * (root * cubic * (p * p) + root))
-        store_cell(cells, xy, 0.5 * p * (1.0 + t))
-        rows = slice(xy * WP, xy * WP + WP)
-        local[xy] = jnp.dot(pw_back, sig[rows], preferred_element_type=F32)[0:W]
-    from_cells(cells, outv)
+    @pl.when(cx < GX)
+    def _():
+        for xy in range(8):
+            p = pre[xy]
+            t = jnp.tanh(p * (root * cubic * (p * p) + root))
+            store_cell(cells, xy, 0.5 * p * (1.0 + t))
+            rows = slice(xy * WP, xy * WP + WP)
+            local[xy] = jnp.dot(pw_back, sig[rows], preferred_element_type=F32)[0:W]
+        from_cells(cells, outv)
+
     drain(c1)
     drain(c2)
     drain(c3)
@@ -417,23 +432,25 @@
     drain(c5)
     drain(c6)
     arrive(c7)
-    arrived = load_cells(v.at[1])
-    for half in range(2):
-        spatial = jnp.dot(unpack_modes(arrived, half), zt[...], preferred_element_type=F32)
-        for sub in range(4):
-            xy = half * 4 + sub
-            store_cell(cells, xy, local[xy] + spatial[sub * WP : sub * WP + W])
+    vout[:, 0:10, :] = v[1, :, 0:10, :]
+    drain(c7)
+
+
+def store_kernel(a, b, v, local, zt, a_out, gfield, b_out, cells, gout, sems):
+    copies = [
+        pltpu.make_async_copy(a, a_out, sems.at[0]),
+        pltpu.make_async_copy(b, b_out, sems.at[1]),
+        pltpu.make_async_copy(gout, gfield, sems.at[2]),
+    ]
+    copies[0].start()
+    copies[1].start()
+    arrived = load_cells(v)
+    both = jnp.concatenate([unpack_modes(arrived, half) for half in range(2)], axis=0)
+    both = jnp.dot(both, zt[...], preferred_element_type=F32)
+    for xy in range(8):
+        store_cell(cells, xy, local[xy] + both[xy * WP : xy * WP + W])
     from_cells(cells, gout)
-    drain(c7)
-
-
-def store_kernel(a, b, c, a_out, b_out, c_out, sems):
-    copies = [
-        pltpu.make_async_copy(src, dst, sems.at[i])
-        for i, (src, dst) in enumerate(((a, a_out), (b, b_out), (c, c_out)))
-    ]
-    for copy in copies:
-        copy.start()
+    copies[2].start()
     for copy in copies:
         copy.wait()
 
@@ -443,19 +460,25 @@
     weight = jnp.transpose(spectral_weight, (0, 1, 2, 4, 5, 3)).reshape(4, 2, W, 16, W)
     hbm = pl.BlockSpec(memory_space=pltpu.MemorySpace.HBM)
     vmem = pl.BlockSpec(memory_space=pltpu.MemorySpace.VMEM)
-    shapes = (((W, 2, 4, Q), BF16), ((W, 2, 4, Q), BF16), ((4, 2, W, 16, W), F32))
+    shapes = (
+        ((W, 2, 4, Q), BF16),
+        ((4, 2, W, 16, W), F32),
+        ((16, 16, 128), F32),
+        ((8, W, Q), F32),
+        ((128, Q), BF16),
+    )
+    field_shape = jax.ShapeDtypeStruct((W, 2, 4, Q), BF16)
     results = pl.pallas_call(
         kernel,
         out_shape=tuple(pltpu.VMEM(shape, dtype) for shape, dtype in shapes),
         in_specs=[hbm] * 10,
-        out_specs=(vmem,) * 3,
+        out_specs=(vmem,) * 5,
         scratch_shapes=[
             pltpu.VMEM((W, 2, 4, Q), BF16),
             pltpu.VMEM((W, 2, 4, Q), BF16),
             pltpu.VMEM((4, 2, W, 16, W), F32),
             pltpu.VMEM((W, W), BF16),
             pltpu.VMEM((W,), F32),
-            pltpu.VMEM((128, Q), BF16),
             pltpu.VMEM((32, 192), BF16),
             pltpu.VMEM((32, 384), BF16),
             pltpu.VMEM((128, 96), BF16),
@@ -465,7 +488,6 @@
             pltpu.VMEM((4, W * 8, 128), F32),
             pltpu.VMEM((128, 128), F32),
             pltpu.VMEM((2, W, 16, 128), F32),
-            pltpu.VMEM((8, W, Q), F32),
             pltpu.VMEM((8, W, Q), F32),
             pltpu.VMEM((256, Q), BF16),
             pltpu.VMEM((32, 128), F32),
@@ -487,11 +509,15 @@
     )(field, cotangent, weight, pointwise_weight, channel_bias, *constants)
     out, gfield, gspec = pl.pallas_call(
         store_kernel,
-        out_shape=tuple(jax.ShapeDtypeStruct(shape, dtype) for shape, dtype in shapes),
-        in_specs=[pl.BlockSpec(memory_space=pl.ANY)] * 3,
+        out_shape=(field_shape, field_shape, jax.ShapeDtypeStruct(*shapes[1])),
+        in_specs=[pl.BlockSpec(memory_space=pl.ANY)] * 2 + [vmem] * 3,
         out_specs=(hbm,) * 3,
-        scratch_shapes=[pltpu.SemaphoreType.DMA((3,))],
-        compiler_params=pltpu.CompilerParams(vmem_limit_bytes=1 << 20),
+        scratch_shapes=[
+            pltpu.VMEM((4, W * 8, 128), F32),
+            pltpu.VMEM((W, 2, 4, Q), BF16),
+            pltpu.SemaphoreType.DMA((3,)),
+        ],
+        compiler_params=pltpu.CompilerParams(vmem_limit_bytes=4 << 20),
     )(*results)
     grad = jnp.transpose(gspec.reshape(4, 2, W, 1, 16, W), (0, 1, 2, 5, 3, 4))
     return out, gfield, grad

time: 55.9 us -> 55.4 us (level)
  Pallas kernels: 55.2 us -> 54.6 us
    pallas_call x1, Pallas kernels: 54 us -> 53.4 us  [on_device(): pl.pallas_call(kernel, out_shape=tuple((pltpu.VMEM(shape, dtype) for shap...]
where the time goes in v10:
time: 55.4 us; the launch traced here: 55.3 us
  Pallas kernels  54.6 us (99%)
  between operations  0.64 us (1%)
    pallas_call x1, Pallas kernels, on_device(): pl.pallas_call(kernel, out_shape=tuple((pltpu.VMEM(shape, dtype) for shap...  53.4 us
    pallas_call x1, Pallas kernels, on_device(): pl.pallas_call(store_kernel, out_shape=(field_shape, field_shape, jax.Sha...  1.24 us

profile of v10, /device:TPU:1, one launch (start us, length us, event | category | flops | bytes accessed | tf_op | source)
XLA Modules:
  0.0 55.3 jit_solution(1865075722257637941)
XLA Ops:
  0.6 53.4 %shard_map.121 = (bf16[20,2,4,512]{3,2,1,0:T(4,128)(2,1)S(1)}, f32[4,2,20,16,20]{4,3,2,1,0:T(8,128)S(1)}, f32[16,16,128]{2,1,0:T(8,128)S(1)}, f32[8,20,512]{2,1,0:T(8,128)S(1)}, bf16[128,512]{1,0:T(8,128)(2,1)S(1)}) custom-call(bf16[20,2,4,512]{3,2,1,0:T(4,128)(2,1)} %field.1, bf16[20,2,4,512]{3,2,1,0:T(4,128)(2,1)} %cot.1, f32[4,2,20,16,20]{4,3,2,1,0:T(8,128)} %bitcast.10, ...), custom_call_target="tpu_custom_call" | custom-call | tf_op jit(solution)/shard_map/pallas_call | solution.py:471
  54.0 1.2 %shard_map.122 = (bf16[20,2,4,512]{3,2,1,0:T(4,128)(2,1)}, bf16[20,2,4,512]{3,2,1,0:T(4,128)(2,1)}, f32[4,2,20,16,20]{4,3,2,1,0:T(8,128)}) custom-call(bf16[20,2,4,512]{3,2,1,0:T(4,128)(2,1)S(1)} %get-tuple-element.11.a, f32[4,2,20,16,20]{4,3,2,1,0:T(8,128)S(1)} %get-tuple-element.12.b, f32[16,16,128]{2,1,0:T(8,128)S(1)} %get-tuple-element.13.v, ...), custom_call_target="tpu_custom_call" | custom-call | tf_op jit(solution)/shard_map/pallas_call | solution.py:510

commit v11 on v10

--- a/solution.py
+++ b/solution.py
@@ -104,7 +104,7 @@
         for sub in range(4)
     ]
     stacked = jnp.concatenate(block_transpose(parts), axis=0)
-    return stacked.T.astype(BF16)
+    return stacked.astype(BF16).T
 
 
 def lanes(i):

time: 55.4 us -> 55.3 us (level)
  no operation moved by 1% of the time
where the time goes in v11:
time: 55.3 us; the launch traced here: 55.2 us
  Pallas kernels  54.6 us (99%)
  between operations  0.64 us (1%)
    pallas_call x1, Pallas kernels, on_device(): pl.pallas_call(kernel, out_shape=tuple((pltpu.VMEM(shape, dtype) for shap...  53.4 us
    pallas_call x1, Pallas kernels, on_device(): pl.pallas_call(store_kernel, out_shape=(field_shape, field_shape, jax.Sha...  1.24 us

profile of v11, /device:TPU:1, one launch (start us, length us, event | category | flops | bytes accessed | tf_op | source)
XLA Modules:
  0.0 55.2 jit_solution(7051670736623964034)
XLA Ops:
  0.6 53.4 %shard_map.121 = (bf16[20,2,4,512]{3,2,1,0:T(4,128)(2,1)S(1)}, f32[4,2,20,16,20]{4,3,2,1,0:T(8,128)S(1)}, f32[16,16,128]{2,1,0:T(8,128)S(1)}, f32[8,20,512]{2,1,0:T(8,128)S(1)}, bf16[128,512]{1,0:T(8,128)(2,1)S(1)}) custom-call(bf16[20,2,4,512]{3,2,1,0:T(4,128)(2,1)} %field.1, bf16[20,2,4,512]{3,2,1,0:T(4,128)(2,1)} %cot.1, f32[4,2,20,16,20]{4,3,2,1,0:T(8,128)} %bitcast.10, ...), custom_call_target="tpu_custom_call" | custom-call | tf_op jit(solution)/shard_map/pallas_call | solution.py:471
  54.0 1.2 %shard_map.122 = (bf16[20,2,4,512]{3,2,1,0:T(4,128)(2,1)}, bf16[20,2,4,512]{3,2,1,0:T(4,128)(2,1)}, f32[4,2,20,16,20]{4,3,2,1,0:T(8,128)}) custom-call(bf16[20,2,4,512]{3,2,1,0:T(4,128)(2,1)S(1)} %get-tuple-element.11.a, f32[4,2,20,16,20]{4,3,2,1,0:T(8,128)S(1)} %get-tuple-element.12.b, f32[16,16,128]{2,1,0:T(8,128)S(1)} %get-tuple-element.13.v, ...), custom_call_target="tpu_custom_call" | custom-call | tf_op jit(solution)/shard_map/pallas_call | solution.py:510
